TPU v7x, 32 devices: a whole 2x2x4 slice. The times are simulated.
32 devices in a mesh: slab: 4 (over z), bulk: 8 (over y, x, core).
Axes of the slice: x: 2, y: 2, z: 4, core: 2. Of those that a mesh axis runs over, the one named last changes fastest.
Arguments:
- atom_counts: int32 [16, 64, 1024], P('slab', 'bulk'), may hold values from 0 to 15
- ion_flags: int32 [16, 64, 1024], P(None, 'bulk', 'slab'), may hold values 0 or 1
- charge_cells: int32 [32768], P(('slab', 'bulk')), may hold values from 0 to 32767
- charge_values: float32 [32768], P(('slab', 'bulk')), may hold values from -16 to 16
Outputs:
- potential: float32 [16, 64, 1024], P(None, 'bulk', 'slab')
- misfit: float32 [16, 64, 1024], P(None, 'bulk', 'slab')
Inputs may be any that keep to these rules, and one draw needn't show every extreme that they name: Entry i of charge_cells is the flat index z * 8 * 256 + x * 256 + y of a cell in the brick of the device that holds entry i; cells may repeat.
All inputs are finite; a program needn't handle non-finite values. No bound on the sum of `ion_flags` on one device may be relied on, other than what follows from the above.
Results may differ from a plain program's by a relative error of at most 0.0001.
Values sent between devices are 32-bit elements; how exact they have to be, the bound alone decides.
A program may use at most 128 MiB of HBM per device.

v0:
```python
import jax
import jax.numpy as jnp
import numpy as np
from jax import lax
from jax.sharding import PartitionSpec as P

GRID_LEVEL_COUNT = 4
COARSE = 8
NEWTON = 2


taper_raw = np.exp(-0.5 * (np.arange(-4, 5) / 1.5) ** 2)
taper_weights = taper_raw / taper_raw.sum()
damping = 0.8
screening = 1.0
density_scale = 2.0


def padded_2(block, sides, width):
    for axis, dim in sides:
        count = lax.axis_size(axis)
        forward = [(i, i + 1) for i in range(count - 1)]
        backward = [(target, source) for source, target in forward]
        low = lax.ppermute(
            lax.slice_in_dim(block, block.shape[dim] - width, None, axis=dim), axis, forward
        )
        high = lax.ppermute(lax.slice_in_dim(block, 0, width, axis=dim), axis, backward)
        block = jnp.concatenate([low, block, high], axis=dim)
    return block


def taper_sum(padded, dimension):
    length = padded.shape[dimension] - 8
    summed = float(taper_weights[0]) * lax.slice_in_dim(padded, 0, length, axis=dimension)
    for offset in range(1, 9):
        summed = summed + float(taper_weights[offset]) * lax.slice_in_dim(
            padded, offset, offset + length, axis=dimension
        )
    return summed


def shifted(padded, dimension, offset):
    starts = [1, 1, 1]
    starts[dimension] = 1 + offset
    limits = [
        starts[0] + padded.shape[0] - 2,
        starts[1] + padded.shape[1] - 2,
        starts[2] + padded.shape[2] - 2,
    ]
    return lax.slice(padded, starts, limits)


def laplace_part(field_pad, dielectric_pad, scaling):
    middle = shifted(field_pad, 0, 0)
    dielectric_mid = shifted(dielectric_pad, 0, 0)
    summed = jnp.zeros_like(middle)
    for dimension in range(3):
        for offset in (-1, 1):
            weight_face = 0.5 * (dielectric_mid + shifted(dielectric_pad, dimension, offset))
            summed = summed + weight_face * (middle - shifted(field_pad, dimension, offset))
    return scaling * summed


def total_face_weight(dielectric_pad, scaling):
    dielectric_mid = shifted(dielectric_pad, 0, 0)
    summed = jnp.zeros_like(dielectric_mid)
    for dimension in range(3):
        for offset in (-1, 1):
            summed = summed + 0.5 * (dielectric_mid + shifted(dielectric_pad, dimension, offset))
    return scaling * summed


def coarsen(values_in):
    sizes_in = values_in.shape
    blocks = values_in.reshape(sizes_in[0] // 2, 2, sizes_in[1] // 2, 2, sizes_in[2] // 2, 2)
    return blocks.sum(axis=(1, 3, 5)) * 0.125


def refine(coarse):
    return jnp.repeat(jnp.repeat(jnp.repeat(coarse, 2, axis=0), 2, axis=1), 2, axis=2)


def rimmed(field_in):
    extended = padded_2(field_in, (("slab", 2), ("bulk", 1)), 1)
    return jnp.pad(extended, ((1, 1), (0, 0), (0, 0)))


def rimmed_dielectric(dielectric_in):
    extended = padded_2(dielectric_in, (("slab", 2), ("bulk", 1)), 1)
    return jnp.pad(extended, ((1, 1), (0, 0), (0, 0)))


def assemble(stacked):
    slab_count = lax.axis_size("slab")
    bulk_count = lax.axis_size("bulk")
    sizes_in = stacked.shape
    blocks = stacked.reshape(slab_count, bulk_count, sizes_in[1], sizes_in[2], sizes_in[3])
    return blocks.transpose(2, 1, 3, 0, 4).reshape(
        sizes_in[1], bulk_count * sizes_in[2], slab_count * sizes_in[3]
    )


def per_device(atom_counts, ion_flags, charge_cells, charge_values):
    density = atom_counts.astype(jnp.float32)
    along_y = taper_sum(jnp.pad(density, ((0, 0), (0, 0), (4, 4))), 2)
    extended = padded_2(along_y, (("slab", 0), ("bulk", 1)), 4)
    slab_shading = jnp.exp(-taper_sum(taper_sum(extended, 0), 1) / density_scale)
    shading = lax.all_to_all(slab_shading, "slab", split_axis=2, concat_axis=0, tiled=True)
    dielectric = 2.0 + 78.0 * shading
    access = shading * shading
    reaction_base = screening * access * (1.0 - ion_flags.astype(jnp.float32))
    flat_source = jnp.zeros((dielectric.size,), jnp.float32).at[charge_cells].add(charge_values)
    source = flat_source.reshape(dielectric.shape)
    dielectrics = [dielectric]
    for grid_height in range(1, GRID_LEVEL_COUNT):
        dielectrics.append(coarsen(dielectrics[-1]))
    scale_factors = [0.25**grid_height for grid_height in range(GRID_LEVEL_COUNT)]
    padded_dielectric_maps = [rimmed_dielectric(item) for item in dielectrics]
    summed_face_weights = [
        total_face_weight(padded_dielectric_maps[grid_height], scale_factors[grid_height])
        for grid_height in range(GRID_LEVEL_COUNT)
    ]
    whole_pad = jnp.pad(
        assemble(lax.all_gather(dielectrics[-1][None], ("slab", "bulk"), axis=0, tiled=True)), 1
    )
    whole_sums = total_face_weight(whole_pad, scale_factors[-1])

    def multigrid(grid_height, target, level_list):
        dielectric_pad, reaction, diagonal, scaling = level_list[grid_height]

        def operate(iterate):
            return laplace_part(rimmed(iterate), dielectric_pad, scaling) + reaction * iterate

        deepest = grid_height == len(level_list) - 1
        if deepest:
            pulled_target, pulled_reaction = (
                lax.all_gather(target[None], ("slab", "bulk"), axis=0, tiled=True),
                lax.all_gather(reaction[None], ("slab", "bulk"), axis=0, tiled=True),
            )
            whole_target = assemble(pulled_target)
            whole_reaction = assemble(pulled_reaction)
            whole_diagonal = whole_sums + whole_reaction
            iterate = damping * whole_target / whole_diagonal
            for repeat in range(COARSE - 1):
                applied = (
                    laplace_part(jnp.pad(iterate, 1), whole_pad, scaling) + whole_reaction * iterate
                )
                iterate = iterate + damping * (whole_target - applied) / whole_diagonal
            anchor = (
                lax.axis_index("bulk") * 0,
                lax.axis_index("bulk") * target.shape[1],
                lax.axis_index("slab") * target.shape[2],
            )
            return lax.dynamic_slice(iterate, anchor, target.shape)
        iterate = damping * target / diagonal
        residue = target - operate(iterate)
        iterate = iterate + refine(multigrid(grid_height + 1, coarsen(residue), level_list))
        iterate = iterate + damping * (target - operate(iterate)) / diagonal
        return iterate

    potential = jnp.zeros_like(dielectric)
    for newton in range(NEWTON):
        if newton == 0:
            misfit = -source
        else:
            misfit = (
                laplace_part(rimmed(potential), padded_dielectric_maps[0], 1.0)
                + reaction_base * jnp.sinh(potential)
                - source
            )
        reaction_terms = [reaction_base * jnp.cosh(potential)]
        for grid_height in range(1, GRID_LEVEL_COUNT):
            reaction_terms.append(coarsen(reaction_terms[-1]))
        level_list = [
            (
                padded_dielectric_maps[grid_height],
                reaction_terms[grid_height],
                summed_face_weights[grid_height] + reaction_terms[grid_height],
                scale_factors[grid_height],
            )
            for grid_height in range(GRID_LEVEL_COUNT)
        ]
        potential = potential + multigrid(0, -misfit, level_list)
    misfit = (
        laplace_part(rimmed(potential), padded_dielectric_maps[0], 1.0)
        + reaction_base * jnp.sinh(potential)
        - source
    )
    return (potential, misfit)


def solution(mesh):
    placed = (
        P("slab", "bulk", None),
        P(None, "bulk", "slab"),
        P(("slab", "bulk")),
        P(("slab", "bulk")),
    )
    return jax.shard_map(
        per_device,
        mesh=mesh,
        in_specs=placed,
        out_specs=(P(None, "bulk", "slab"), P(None, "bulk", "slab")),
        check_vma=False,
    )
```

profile of v0, /device:TPU:0, one launch (start us, length us, event | category | flops | bytes accessed | tf_op | source)
XLA Modules:
  0.0 577.2 jit_solution(675253163761681293)
XLA Ops:
  3.2 5.6 collective-permute-start
  13.2 3.0 collective-permute-start.2
  18.8 3.1 reshape.282
  21.9 5.9 %all-to-all-start = ((f32[4,1,8192]{2,1,0:T(1,128)}), f32[4,1,8192]{2,1,0:T(1,128)S(1)}, u32[]{:S(2)}, u32[]{:S(2)}) async-start(f32[4,1,8192]{2,1,0:T(1,128)} %reshape.282), calls=%async_computation | async-start | bytes 262144 | tf_op jit(solution)/shard_map/all_to_all | solution.py:108
  27.8 6.1 %scatter_custom_fusion = f32[32768]{0:T(1024)S(1)} fusion(s32[1024]{0:T(1024)S(1)} %compare_select_fusion, f32[1024]{0:T(1024)} %param.7, f32[]{:T(128)} %constant.24.clone.1), kind=kCustom, calls=%fused_computation.403 | custom fusion | flops 1024 | bytes 131584 | tf_op jit(solution)/shard_map/scatter-add | solution.py:112
  35.5 2.5 reshape.283
  39.0 9.8 %add.1133 = f32[8,2,4,2,128,2]{5,4,3,2,1,0:T(8,128)} reshape(f32[4,4,8,256]{3,2,1,0:T(8,128)S(1)} %copy.339) | data formatting | bytes 262144 | tf_op jit(solution)/shard_map/add | solution.py:109
  48.8 4.1 reduce_sum.171
  53.1 3.9 collective-permute-start.4
  58.3 4.5 collective-permute-start.12
  65.4 4.5 collective-permute-start.20
  72.6 4.5 collective-permute-done.21
  80.2 8.7 %collective-permute-start.6 = (f32[16,1,258]{2,1,0:T(1,128)S(1)}, f32[16,1,258]{2,1,0:T(1,128)S(1)}, u32[]{:S(2)}, u32[]{:S(2)}) collective-permute-start(f32[16,1,258]{2,1,0:T(1,128)S(1)} %get-tuple-element.59), channel_id=1, source_target_pairs={{0,1},{1,2},{2,3},{3,4},{4,5},{5,6},{6,7},{8,9},{9,10},{10,11},{11... | collective-permute-start | bytes 49544 | tf_op jit(solution)/shard_map/ppermute | solution.py:24
  90.3 4.3 collective-permute-start.14
  96.8 3.9 collective-permute-start.8
  102.6 4.3 collective-permute-done.9
  107.1 2.8 collective-permute-start.10
  111.3 9.8 %reshape.219 = f32[8,2,4,2,128,2]{5,4,3,2,1,0:T(8,128)} reshape(f32[16,8,256]{2,1,0:T(8,128)S(1)} %get-tuple-element.37) | data formatting | bytes 262144 | tf_op jit(solution)/shard_map/reshape | solution.py:75
  121.1 4.0 reduce_sum.172
  125.7 9.8 %reshape.218 = f32[8,2,4,2,128,2]{5,4,3,2,1,0:T(8,128)} reshape(f32[16,8,256]{2,1,0:T(8,128)S(1)} %fusion.127) | data formatting | bytes 262144 | tf_op jit(solution)/shard_map/reshape | solution.py:75
  135.5 4.0 reduce_sum.170
  139.8 3.4 collective-permute-start.16
  144.6 4.2 collective-permute-done.17
  148.9 4.3 collective-permute-start.18
  156.3 2.6 collective-permute-done.19
  164.9 42.3 %all-gather.6 = f32[32,2,32]{2,1,0:T(2,128)S(1)} all-gather(f32[1,2,32]{2,1,0:T(2,128)S(1)} %multiply_bitcast_fusion.3), channel_id=3, replica_groups=mesh['slab'=4,'bulk'=8] {'slab','bulk'}, dimensions={0}, use_global_device_ids=true | all-gather | bytes 8448 | tf_op jit(solution)/shard_map/all_gather | solution.py:124
  207.5 2.2 collective-permute-start.26
  211.0 39.5 %all-gather.7 = f32[32,2,32]{2,1,0:T(2,128)S(1)} all-gather(f32[1,2,32]{2,1,0:T(2,128)S(1)} %multiply_bitcast_fusion.2), channel_id=4, replica_groups=mesh['slab'=4,'bulk'=8] {'slab','bulk'}, dimensions={0}, use_global_device_ids=true | all-gather | bytes 8448 | tf_op jit(solution)/shard_map/all_gather | solution.py:138
  251.1 36.6 %all-gather.5 = f32[32,2,32]{2,1,0:T(2,128)S(1)} all-gather(f32[1,2,32]{2,1,0:T(2,128)S(1)} %multiply_bitcast_fusion.4), channel_id=2, replica_groups=mesh['slab'=4,'bulk'=8] {'slab','bulk'}, dimensions={0}, use_global_device_ids=true | all-gather | bytes 8448 | tf_op jit(solution)/shard_map/all_gather | solution.py:137
  292.1 4.2 collective-permute-done.29
  298.9 3.7 collective-permute-done.31
  306.4 4.2 collective-permute-done.33
  310.7 2.8 collective-permute-start.34
  314.8 2.9 collective-permute-done.35
  323.4 4.3 collective-permute-done.37
  327.8 2.9 collective-permute-start.38
  330.7 11.1 %collective-permute-start.39 = (f32[16,1,258]{2,1,0:T(1,128)S(1)}, f32[16,1,258]{2,1,0:T(1,128)S(1)}, u32[]{:S(2)}, u32[]{:S(2)}) collective-permute-start(f32[16,1,258]{2,1,0:T(1,128)S(1)} %get-tuple-element.56), channel_id=1, source_target_pairs={{1,0},{2,1},{3,2},{4,3},{5,4},{6,5},{7,6},{9,8},{10,9},{11,10},{12... | collective-permute-start | bytes 49544 | tf_op jit(solution)/shard_map/ppermute | solution.py:27
  346.6 4.3 collective-permute-done.41
  351.1 2.8 collective-permute-start.42
  355.2 5.1 collective-permute-done.43
  364.6 4.3 collective-permute-done.45
  369.0 3.2 collective-permute-start.46
  373.6 9.8 %reshape.234 = f32[8,2,4,2,128,2]{5,4,3,2,1,0:T(8,128)} reshape(f32[16,8,256]{2,1,0:T(8,128)S(1)} %get-tuple-element.9) | data formatting | bytes 262144 | tf_op jit(solution)/shard_map/reshape | solution.py:75
  383.3 4.0 reduce_sum.186
  388.0 9.8 %reshape.233 = f32[8,2,4,2,128,2]{5,4,3,2,1,0:T(8,128)} reshape(f32[16,8,256]{2,1,0:T(8,128)S(1)} %fusion.75) | data formatting | bytes 262144 | tf_op jit(solution)/shard_map/reshape | solution.py:75
  397.9 4.0 reduce_sum.185
  405.6 4.2 collective-permute-done.49
  409.9 4.0 collective-permute-start.50
  416.4 3.9 collective-permute-done.51
  425.3 4.0 collective-permute-done.53
  429.3 2.9 collective-permute-start.54
  433.5 41.6 %all-gather.9 = f32[32,2,32]{2,1,0:T(2,128)S(1)} all-gather(f32[1,2,32]{2,1,0:T(2,128)S(1)} %multiply_bitcast_fusion), channel_id=6, replica_groups=mesh['slab'=4,'bulk'=8] {'slab','bulk'}, dimensions={0}, use_global_device_ids=true | all-gather | bytes 8448 | tf_op jit(solution)/shard_map/all_gather | solution.py:138
  475.6 36.7 %all-gather.8 = f32[32,2,32]{2,1,0:T(2,128)S(1)} all-gather(f32[1,2,32]{2,1,0:T(2,128)S(1)} %multiply_bitcast_fusion.1), channel_id=5, replica_groups=mesh['slab'=4,'bulk'=8] {'slab','bulk'}, dimensions={0}, use_global_device_ids=true | all-gather | bytes 8448 | tf_op jit(solution)/shard_map/all_gather | solution.py:137
  516.0 4.2 collective-permute-done.57
  522.9 3.6 collective-permute-done.59
  530.2 4.2 collective-permute-done.61
  534.5 2.8 collective-permute-start.62
  538.6 2.9 collective-permute-done.63
  546.4 4.3 collective-permute-done.65
  550.9 2.9 collective-permute-start.66
  555.1 3.3 collective-permute-done.67
  562.8 4.3 collective-permute-done.69
  567.3 3.4 collective-permute-start.70
  572.1 3.7 collective-permute-done.71
  (393 shorter events, 109.9 us)
Async XLA Ops:
  1.9 8.4 %collective-permute-start.1 = (f32[4,8,1024]{2,1,0:T(8,128)S(1)}, f32[4,8,1024]{2,1,0:T(8,128)S(1)}, u32[]{:S(2)}, u32[]{:S(2)}) collective-permute-start(f32[4,8,1024]{2,1,0:T(8,128)S(1)} %fusion.17), channel_id=1, source_target_pairs={{8,0},{16,8},{24,16},{9,1},{17,9},{25,17},{10,2},{18,10},{26,18},{... | collective-permute-start | bytes 393224 | tf_op jit(solution)/shard_map/ppermute | solution.py:27
  3.2 8.3 %collective-permute-start = (f32[4,8,1024]{2,1,0:T(8,128)S(1)}, f32[4,8,1024]{2,1,0:T(8,128)S(1)}, u32[]{:S(2)}, u32[]{:S(2)}) collective-permute-start(f32[4,8,1024]{2,1,0:T(8,128)S(1)} %fusion.17), channel_id=1, source_target_pairs={{0,8},{8,16},{16,24},{1,9},{9,17},{17,25},{2,10},{10,18},{18,26},{... | collective-permute-start | bytes 393224 | tf_op jit(solution)/shard_map/ppermute | solution.py:24
  11.8 4.5 collective-permute-start.3
  13.2 4.2 collective-permute-start.2
  21.9 12.1 %all-to-all-start = ((f32[4,1,8192]{2,1,0:T(1,128)}), f32[4,1,8192]{2,1,0:T(1,128)S(1)}, u32[]{:S(2)}, u32[]{:S(2)}) async-start(f32[4,1,8192]{2,1,0:T(1,128)} %reshape.282), calls=%async_computation | async-start | bytes 262144 | tf_op jit(solution)/shard_map/all_to_all | solution.py:108
  53.1 26.9 %collective-permute-start.4 = (f32[16,8,1]{2,1,0:T(8,128)S(1)}, f32[16,8,1]{2,1,0:T(8,128)S(1)}, u32[]{:S(2)}, u32[]{:S(2)}) collective-permute-start(f32[16,8,1]{2,1,0:T(8,128)S(1)} %get-tuple-element.75), channel_id=1, source_target_pairs={{0,8},{8,16},{16,24},{1,9},{9,17},{17,25},{2,10},{10,18},{18,26},{... | collective-permute-start | bytes 1544 | tf_op jit(solution)/shard_map/ppermute | solution.py:24
  57.0 22.9 %collective-permute-start.5 = (f32[16,8,1]{2,1,0:T(8,128)S(1)}, f32[16,8,1]{2,1,0:T(8,128)S(1)}, u32[]{:S(2)}, u32[]{:S(2)}) collective-permute-start(f32[16,8,1]{2,1,0:T(8,128)S(1)} %get-tuple-element.76), channel_id=1, source_target_pairs={{8,0},{16,8},{24,16},{9,1},{17,9},{25,17},{10,2},{18,10},{26,18},{... | collective-permute-start | bytes 1544 | tf_op jit(solution)/shard_map/ppermute | solution.py:27
  58.3 20.3 %collective-permute-start.12 = (f32[8,4,1]{2,1,0:T(4,128)S(1)}, f32[8,4,1]{2,1,0:T(4,128)S(1)}, u32[]{:S(2)}, u32[]{:S(2)}) collective-permute-start(f32[8,4,1]{2,1,0:T(4,128)S(1)} %get-tuple-element.108), channel_id=1, source_target_pairs={{0,8},{8,16},{16,24},{1,9},{9,17},{17,25},{2,10},{10,18},{18,26},{... | collective-permute-start | bytes 392 | tf_op jit(solution)/shard_map/ppermute | solution.py:24
  62.9 17.1 %collective-permute-start.13 = (f32[8,4,1]{2,1,0:T(4,128)S(1)}, f32[8,4,1]{2,1,0:T(4,128)S(1)}, u32[]{:S(2)}, u32[]{:S(2)}) collective-permute-start(f32[8,4,1]{2,1,0:T(4,128)S(1)} %get-tuple-element.109), channel_id=1, source_target_pairs={{8,0},{16,8},{24,16},{9,1},{17,9},{25,17},{10,2},{18,10},{26,18},{... | collective-permute-start | bytes 392 | tf_op jit(solution)/shard_map/ppermute | solution.py:27
  65.4 5.9 %collective-permute-start.20 = (f32[4,2,1]{2,0,1:T(4,128)S(1)}, f32[4,2,1]{2,0,1:T(4,128)S(1)}, u32[]{:S(2)}, u32[]{:S(2)}) collective-permute-start(f32[4,2,1]{2,0,1:T(4,128)S(1)} %get-tuple-element.132), channel_id=1, source_target_pairs={{0,8},{8,16},{16,24},{1,9},{9,17},{17,25},{2,10},{10,18},{18,26},{... | collective-permute-start | bytes 104 | tf_op jit(solution)/shard_map/ppermute | solution.py:24
  71.3 5.8 collective-permute-start.21
  77.1 77.4 %collective-permute-start.22 = (f32[4,1,66]{2,0,1:T(4,128)S(1)}, f32[4,1,66]{2,0,1:T(4,128)S(1)}, u32[]{:S(2)}, u32[]{:S(2)}) collective-permute-start(f32[4,1,66]{2,0,1:T(4,128)S(1)} %get-tuple-element.130), channel_id=1, source_target_pairs={{0,1},{1,2},{2,3},{3,4},{4,5},{5,6},{6,7},{8,9},{9,10},{10,11},{11... | collective-permute-start | bytes 3176 | tf_op jit(solution)/shard_map/ppermute | solution.py:24
  78.6 75.9 %collective-permute-start.23 = (f32[4,1,66]{2,0,1:T(4,128)S(1)}, f32[4,1,66]{2,0,1:T(4,128)S(1)}, u32[]{:S(2)}, u32[]{:S(2)}) collective-permute-start(f32[4,1,66]{2,0,1:T(4,128)S(1)} %get-tuple-element.131), channel_id=1, source_target_pairs={{1,0},{2,1},{3,2},{4,3},{5,4},{6,5},{7,6},{9,8},{10,9},{11,10},{12... | collective-permute-start | bytes 3176 | tf_op jit(solution)/shard_map/ppermute | solution.py:27
  80.2 14.4 %collective-permute-start.6 = (f32[16,1,258]{2,1,0:T(1,128)S(1)}, f32[16,1,258]{2,1,0:T(1,128)S(1)}, u32[]{:S(2)}, u32[]{:S(2)}) collective-permute-start(f32[16,1,258]{2,1,0:T(1,128)S(1)} %get-tuple-element.59), channel_id=1, source_target_pairs={{0,1},{1,2},{2,3},{3,4},{4,5},{5,6},{6,7},{8,9},{9,10},{10,11},{11... | collective-permute-start | bytes 49544 | tf_op jit(solution)/shard_map/ppermute | solution.py:24
  88.9 7.2 %collective-permute-start.7 = (f32[16,1,258]{2,1,0:T(1,128)S(1)}, f32[16,1,258]{2,1,0:T(1,128)S(1)}, u32[]{:S(2)}, u32[]{:S(2)}) collective-permute-start(f32[16,1,258]{2,1,0:T(1,128)S(1)} %get-tuple-element.60), channel_id=1, source_target_pairs={{1,0},{2,1},{3,2},{4,3},{5,4},{6,5},{7,6},{9,8},{10,9},{11,10},{12... | collective-permute-start | bytes 49544 | tf_op jit(solution)/shard_map/ppermute | solution.py:27
  90.3 10.4 %collective-permute-start.14 = (f32[8,1,130]{2,0,1:T(8,128)S(1)}, f32[8,1,130]{2,0,1:T(8,128)S(1)}, u32[]{:S(2)}, u32[]{:S(2)}) collective-permute-start(f32[8,1,130]{2,0,1:T(8,128)S(1)} %get-tuple-element.95), channel_id=1, source_target_pairs={{0,1},{1,2},{2,3},{3,4},{4,5},{5,6},{6,7},{8,9},{9,10},{10,11},{11... | collective-permute-start | bytes 12488 | tf_op jit(solution)/shard_map/ppermute | solution.py:24
  94.6 7.5 %collective-permute-start.15 = (f32[8,1,130]{2,0,1:T(8,128)S(1)}, f32[8,1,130]{2,0,1:T(8,128)S(1)}, u32[]{:S(2)}, u32[]{:S(2)}) collective-permute-start(f32[8,1,130]{2,0,1:T(8,128)S(1)} %get-tuple-element.96), channel_id=1, source_target_pairs={{1,0},{2,1},{3,2},{4,3},{5,4},{6,5},{7,6},{9,8},{10,9},{11,10},{12... | collective-permute-start | bytes 12488 | tf_op jit(solution)/shard_map/ppermute | solution.py:27
  96.8 5.8 %collective-permute-start.8 = (f32[16,8,1]{2,1,0:T(8,128)S(1)}, f32[16,8,1]{2,1,0:T(8,128)S(1)}, u32[]{:S(2)}, u32[]{:S(2)}) collective-permute-start(f32[16,8,1]{2,1,0:T(8,128)S(1)} %get-tuple-element.73), channel_id=1, source_target_pairs={{0,8},{8,16},{16,24},{1,9},{9,17},{17,25},{2,10},{10,18},{18,26},{... | collective-permute-start | bytes 1544 | tf_op jit(solution)/shard_map/ppermute | solution.py:24
  100.7 6.2 %collective-permute-start.9 = (f32[16,8,1]{2,1,0:T(8,128)S(1)}, f32[16,8,1]{2,1,0:T(8,128)S(1)}, u32[]{:S(2)}, u32[]{:S(2)}) collective-permute-start(f32[16,8,1]{2,1,0:T(8,128)S(1)} %get-tuple-element.74), channel_id=1, source_target_pairs={{8,0},{16,8},{24,16},{9,1},{17,9},{25,17},{10,2},{18,10},{26,18},{... | collective-permute-start | bytes 1544 | tf_op jit(solution)/shard_map/ppermute | solution.py:27
  107.1 18.1 %collective-permute-start.10 = (f32[16,1,258]{2,1,0:T(1,128)S(1)}, f32[16,1,258]{2,1,0:T(1,128)S(1)}, u32[]{:S(2)}, u32[]{:S(2)}) collective-permute-start(f32[16,1,258]{2,1,0:T(1,128)S(1)} %get-tuple-element.57), channel_id=1, source_target_pairs={{0,1},{1,2},{2,3},{3,4},{4,5},{5,6},{6,7},{8,9},{9,10},{10,11},{11... | collective-permute-start | bytes 49544 | tf_op jit(solution)/shard_map/ppermute | solution.py:24
  109.9 15.2 %collective-permute-start.11 = (f32[16,1,258]{2,1,0:T(1,128)S(1)}, f32[16,1,258]{2,1,0:T(1,128)S(1)}, u32[]{:S(2)}, u32[]{:S(2)}) collective-permute-start(f32[16,1,258]{2,1,0:T(1,128)S(1)} %get-tuple-element.58), channel_id=1, source_target_pairs={{1,0},{2,1},{3,2},{4,3},{5,4},{6,5},{7,6},{9,8},{10,9},{11,10},{12... | collective-permute-start | bytes 49544 | tf_op jit(solution)/shard_map/ppermute | solution.py:27
  139.8 4.8 collective-permute-start.16
  143.2 5.6 collective-permute-start.17
  148.9 7.4 %collective-permute-start.18 = (f32[8,1,130]{2,0,1:T(8,128)S(1)}, f32[8,1,130]{2,0,1:T(8,128)S(1)}, u32[]{:S(2)}, u32[]{:S(2)}) collective-permute-start(f32[8,1,130]{2,0,1:T(8,128)S(1)} %get-tuple-element.91), channel_id=1, source_target_pairs={{0,1},{1,2},{2,3},{3,4},{4,5},{5,6},{6,7},{8,9},{9,10},{10,11},{11... | collective-permute-start | bytes 12488 | tf_op jit(solution)/shard_map/ppermute | solution.py:24
  153.2 5.7 collective-permute-start.19
  161.4 45.9 %collective-permute-start.24 = (f32[4,2,1]{2,0,1:T(4,128)S(1)}, f32[4,2,1]{2,0,1:T(4,128)S(1)}, u32[]{:S(2)}, u32[]{:S(2)}) collective-permute-start(f32[4,2,1]{2,0,1:T(4,128)S(1)} %get-tuple-element.128), channel_id=1, source_target_pairs={{0,8},{8,16},{16,24},{1,9},{9,17},{17,25},{2,10},{10,18},{18,26},{... | collective-permute-start | bytes 104 | tf_op jit(solution)/shard_map/ppermute | solution.py:24
  163.4 44.0 %collective-permute-start.25 = (f32[4,2,1]{2,0,1:T(4,128)S(1)}, f32[4,2,1]{2,0,1:T(4,128)S(1)}, u32[]{:S(2)}, u32[]{:S(2)}) collective-permute-start(f32[4,2,1]{2,0,1:T(4,128)S(1)} %get-tuple-element.129), channel_id=1, source_target_pairs={{8,0},{16,8},{24,16},{9,1},{17,9},{25,17},{10,2},{18,10},{26,18},{... | collective-permute-start | bytes 104 | tf_op jit(solution)/shard_map/ppermute | solution.py:27
  207.5 43.2 %collective-permute-start.26 = (f32[4,1,66]{2,0,1:T(4,128)S(1)}, f32[4,1,66]{2,0,1:T(4,128)S(1)}, u32[]{:S(2)}, u32[]{:S(2)}) collective-permute-start(f32[4,1,66]{2,0,1:T(4,128)S(1)} %get-tuple-element.126), channel_id=1, source_target_pairs={{0,1},{1,2},{2,3},{3,4},{4,5},{5,6},{6,7},{8,9},{9,10},{10,11},{11... | collective-permute-start | bytes 3176 | tf_op jit(solution)/shard_map/ppermute | solution.py:24
  209.7 41.0 %collective-permute-start.27 = (f32[4,1,66]{2,0,1:T(4,128)S(1)}, f32[4,1,66]{2,0,1:T(4,128)S(1)}, u32[]{:S(2)}, u32[]{:S(2)}) collective-permute-start(f32[4,1,66]{2,0,1:T(4,128)S(1)} %get-tuple-element.127), channel_id=1, source_target_pairs={{1,0},{2,1},{3,2},{4,3},{5,4},{6,5},{7,6},{9,8},{10,9},{11,10},{12... | collective-permute-start | bytes 3176 | tf_op jit(solution)/shard_map/ppermute | solution.py:27
  290.8 5.5 collective-permute-start.29
  297.6 5.0 collective-permute-start.31
  305.0 5.6 collective-permute-start.33
  310.7 4.1 collective-permute-start.34
  313.5 4.2 collective-permute-start.35
  319.7 3.7 collective-permute-start.36
  321.5 6.2 %collective-permute-start.37 = (f32[16,8,1]{2,1,0:T(8,128)S(1)}, f32[16,8,1]{2,1,0:T(8,128)S(1)}, u32[]{:S(2)}, u32[]{:S(2)}) collective-permute-start(f32[16,8,1]{2,1,0:T(8,128)S(1)} %get-tuple-element.72), channel_id=1, source_target_pairs={{8,0},{16,8},{24,16},{9,1},{17,9},{25,17},{10,2},{18,10},{26,18},{... | collective-permute-start | bytes 1544 | tf_op jit(solution)/shard_map/ppermute | solution.py:27
  327.8 14.0 %collective-permute-start.38 = (f32[16,1,258]{2,1,0:T(1,128)S(1)}, f32[16,1,258]{2,1,0:T(1,128)S(1)}, u32[]{:S(2)}, u32[]{:S(2)}) collective-permute-start(f32[16,1,258]{2,1,0:T(1,128)S(1)} %get-tuple-element.55), channel_id=1, source_target_pairs={{0,1},{1,2},{2,3},{3,4},{4,5},{5,6},{6,7},{8,9},{9,10},{10,11},{11... | collective-permute-start | bytes 49544 | tf_op jit(solution)/shard_map/ppermute | solution.py:24
  330.7 11.1 %collective-permute-start.39 = (f32[16,1,258]{2,1,0:T(1,128)S(1)}, f32[16,1,258]{2,1,0:T(1,128)S(1)}, u32[]{:S(2)}, u32[]{:S(2)}) collective-permute-start(f32[16,1,258]{2,1,0:T(1,128)S(1)} %get-tuple-element.56), channel_id=1, source_target_pairs={{1,0},{2,1},{3,2},{4,3},{5,4},{6,5},{7,6},{9,8},{10,9},{11,10},{12... | collective-permute-start | bytes 49544 | tf_op jit(solution)/shard_map/ppermute | solution.py:27
  342.5 4.1 collective-permute-start.40
  344.7 6.2 %collective-permute-start.41 = (f32[16,8,1]{2,1,0:T(8,128)S(1)}, f32[16,8,1]{2,1,0:T(8,128)S(1)}, u32[]{:S(2)}, u32[]{:S(2)}) collective-permute-start(f32[16,8,1]{2,1,0:T(8,128)S(1)} %get-tuple-element.70), channel_id=1, source_target_pairs={{8,0},{16,8},{24,16},{9,1},{17,9},{25,17},{10,2},{18,10},{26,18},{... | collective-permute-start | bytes 1544 | tf_op jit(solution)/shard_map/ppermute | solution.py:27
  351.1 4.1 collective-permute-start.42
  353.9 6.4 %collective-permute-start.43 = (f32[16,1,258]{2,1,0:T(1,128)S(1)}, f32[16,1,258]{2,1,0:T(1,128)S(1)}, u32[]{:S(2)}, u32[]{:S(2)}) collective-permute-start(f32[16,1,258]{2,1,0:T(1,128)S(1)} %get-tuple-element.54), channel_id=1, source_target_pairs={{1,0},{2,1},{3,2},{4,3},{5,4},{6,5},{7,6},{9,8},{10,9},{11,10},{12... | collective-permute-start | bytes 49544 | tf_op jit(solution)/shard_map/ppermute | solution.py:27
  362.7 6.2 %collective-permute-start.45 = (f32[16,8,1]{2,1,0:T(8,128)S(1)}, f32[16,8,1]{2,1,0:T(8,128)S(1)}, u32[]{:S(2)}, u32[]{:S(2)}) collective-permute-start(f32[16,8,1]{2,1,0:T(8,128)S(1)} %get-tuple-element.68), channel_id=1, source_target_pairs={{8,0},{16,8},{24,16},{9,1},{17,9},{25,17},{10,2},{18,10},{26,18},{... | collective-permute-start | bytes 1544 | tf_op jit(solution)/shard_map/ppermute | solution.py:27
  369.0 18.3 %collective-permute-start.46 = (f32[16,1,258]{2,1,0:T(1,128)S(1)}, f32[16,1,258]{2,1,0:T(1,128)S(1)}, u32[]{:S(2)}, u32[]{:S(2)}) collective-permute-start(f32[16,1,258]{2,1,0:T(1,128)S(1)} %get-tuple-element.51), channel_id=1, source_target_pairs={{0,1},{1,2},{2,3},{3,4},{4,5},{5,6},{6,7},{8,9},{9,10},{10,11},{11... | collective-permute-start | bytes 49544 | tf_op jit(solution)/shard_map/ppermute | solution.py:24
  372.3 15.1 %collective-permute-start.47 = (f32[16,1,258]{2,1,0:T(1,128)S(1)}, f32[16,1,258]{2,1,0:T(1,128)S(1)}, u32[]{:S(2)}, u32[]{:S(2)}) collective-permute-start(f32[16,1,258]{2,1,0:T(1,128)S(1)} %get-tuple-element.52), channel_id=1, source_target_pairs={{1,0},{2,1},{3,2},{4,3},{5,4},{6,5},{7,6},{9,8},{10,9},{11,10},{12... | collective-permute-start | bytes 49544 | tf_op jit(solution)/shard_map/ppermute | solution.py:27
  404.2 5.6 collective-permute-start.49
  409.9 6.5 %collective-permute-start.50 = (f32[8,1,130]{2,0,1:T(8,128)S(1)}, f32[8,1,130]{2,0,1:T(8,128)S(1)}, u32[]{:S(2)}, u32[]{:S(2)}) collective-permute-start(f32[8,1,130]{2,0,1:T(8,128)S(1)} %get-tuple-element.83), channel_id=1, source_target_pairs={{0,1},{1,2},{2,3},{3,4},{4,5},{5,6},{6,7},{8,9},{9,10},{10,11},{11... | collective-permute-start | bytes 12488 | tf_op jit(solution)/shard_map/ppermute | solution.py:24
  413.9 6.4 %collective-permute-start.51 = (f32[8,1,130]{2,0,1:T(8,128)S(1)}, f32[8,1,130]{2,0,1:T(8,128)S(1)}, u32[]{:S(2)}, u32[]{:S(2)}) collective-permute-start(f32[8,1,130]{2,0,1:T(8,128)S(1)} %get-tuple-element.84), channel_id=1, source_target_pairs={{1,0},{2,1},{3,2},{4,3},{5,4},{6,5},{7,6},{9,8},{10,9},{11,10},{12... | collective-permute-start | bytes 12488 | tf_op jit(solution)/shard_map/ppermute | solution.py:27
  423.8 5.5 collective-permute-start.53
  429.3 45.8 %collective-permute-start.54 = (f32[4,1,66]{2,0,1:T(4,128)S(1)}, f32[4,1,66]{2,0,1:T(4,128)S(1)}, u32[]{:S(2)}, u32[]{:S(2)}) collective-permute-start(f32[4,1,66]{2,0,1:T(4,128)S(1)} %get-tuple-element.116), channel_id=1, source_target_pairs={{0,1},{1,2},{2,3},{3,4},{4,5},{5,6},{6,7},{8,9},{9,10},{10,11},{11... | collective-permute-start | bytes 3176 | tf_op jit(solution)/shard_map/ppermute | solution.py:24
  432.2 43.0 %collective-permute-start.55 = (f32[4,1,66]{2,0,1:T(4,128)S(1)}, f32[4,1,66]{2,0,1:T(4,128)S(1)}, u32[]{:S(2)}, u32[]{:S(2)}) collective-permute-start(f32[4,1,66]{2,0,1:T(4,128)S(1)} %get-tuple-element.117), channel_id=1, source_target_pairs={{1,0},{2,1},{3,2},{4,3},{5,4},{6,5},{7,6},{9,8},{10,9},{11,10},{12... | collective-permute-start | bytes 3176 | tf_op jit(solution)/shard_map/ppermute | solution.py:27
  514.7 5.5 collective-permute-start.57
  521.6 4.9 collective-permute-start.59
  528.8 5.6 collective-permute-start.61
  534.5 4.1 collective-permute-start.62
  537.3 4.2 collective-permute-start.63
  542.7 3.7 collective-permute-start.64
  544.5 6.2 %collective-permute-start.65 = (f32[16,8,1]{2,1,0:T(8,128)S(1)}, f32[16,8,1]{2,1,0:T(8,128)S(1)}, u32[]{:S(2)}, u32[]{:S(2)}) collective-permute-start(f32[16,8,1]{2,1,0:T(8,128)S(1)} %get-tuple-element.66), channel_id=1, source_target_pairs={{8,0},{16,8},{24,16},{9,1},{17,9},{25,17},{10,2},{18,10},{26,18},{... | collective-permute-start | bytes 1544 | tf_op jit(solution)/shard_map/ppermute | solution.py:27
  550.9 4.2 collective-permute-start.66
  553.8 4.6 collective-permute-start.67
  559.0 3.8 collective-permute-start.68
  561.0 6.2 %collective-permute-start.69 = (f32[16,8,1]{2,1,0:T(8,128)S(1)}, f32[16,8,1]{2,1,0:T(8,128)S(1)}, u32[]{:S(2)}, u32[]{:S(2)}) collective-permute-start(f32[16,8,1]{2,1,0:T(8,128)S(1)} %get-tuple-element.64), channel_id=1, source_target_pairs={{8,0},{16,8},{24,16},{9,1},{17,9},{25,17},{10,2},{18,10},{26,18},{... | collective-permute-start | bytes 1544 | tf_op jit(solution)/shard_map/ppermute | solution.py:27
  567.3 4.8 collective-permute-start.70
  570.8 5.0 collective-permute-start.71
  (46 other events, 3247.4 us)
where the time goes:
time: 588 us; the launch traced here: 577 us
  blocking collectives  197 us (34%)
  starting transfers between devices  167 us (28%)
  waiting for transfers between devices  100 us (17%)
  local copies, waits for them, and re-layouts  68.2 us (12%)
  other arithmetic  42.9 us (7%)
    ppermute x36, starting transfers between devices, padded_2(): lax.ppermute(lax.slice_in_dim(block, block.shape[dim] - width, None, axis...  104 us
    ppermute x36, waiting for transfers between devices, padded_2(): lax.ppermute(lax.slice_in_dim(block, 0, width, axis=dim), axis, backward)  92.5 us
    all_gather x2, blocking collectives, multigrid(): lax.all_gather(reaction[None], ('slab', 'bulk'), axis=0, tiled=True)  81 us
    all_gather x2, blocking collectives, multigrid(): lax.all_gather(target[None], ('slab', 'bulk'), axis=0, tiled=True)  73.4 us
    ppermute x36, starting transfers between devices, padded_2(): lax.ppermute(lax.slice_in_dim(block, 0, width, axis=dim), axis, backward)  56.6 us
    all_gather x1, blocking collectives, per_device(): lax.all_gather(dielectrics[-1][None], ('slab', 'bulk'), axis=0, tiled=True)  42.3 us
    reshape x6, local copies, waits for them, and re-layouts, coarsen(): values_in.reshape(sizes_in[0] // 2, 2, sizes_in[1] // 2, 2, sizes_in[2] /...  41.2 us
    reduce_sum x18, other arithmetic, coarsen(): return blocks.sum(axis=(1, 3, 5)) * 0.125  21.6 us
  transfers between devices with their start and end apart: 73, of which 37 were waited for; matrix products, arithmetic and copies ran while one was open for 9% of the time, Pallas kernels for 0%

commit v1 on v0

v1 whole, which is shorter than its diff:
```python
import jax
import jax.numpy as jnp
import numpy as np
from jax import lax
from jax.experimental import pallas as pl
from jax.experimental.pallas import tpu as pltpu
from jax.sharding import PartitionSpec as P

GRID_LEVEL_COUNT = 4
COARSE = 8
NEWTON = 2


taper_raw = np.exp(-0.5 * (np.arange(-4, 5) / 1.5) ** 2)
taper_weights = taper_raw / taper_raw.sum()
damping = 0.8
screening = 1.0
density_scale = 2.0


def padded_2(block, sides, width):
    for axis, dim in sides:
        count = lax.axis_size(axis)
        forward = [(i, i + 1) for i in range(count - 1)]
        backward = [(target, source) for source, target in forward]
        low = lax.ppermute(
            lax.slice_in_dim(block, block.shape[dim] - width, None, axis=dim), axis, forward
        )
        high = lax.ppermute(lax.slice_in_dim(block, 0, width, axis=dim), axis, backward)
        block = jnp.concatenate([low, block, high], axis=dim)
    return block


def taper_sum(padded, dimension):
    length = padded.shape[dimension] - 8
    summed = float(taper_weights[0]) * lax.slice_in_dim(padded, 0, length, axis=dimension)
    for offset in range(1, 9):
        summed = summed + float(taper_weights[offset]) * lax.slice_in_dim(
            padded, offset, offset + length, axis=dimension
        )
    return summed


MESH_ID = pl.DeviceIdType.MESH
LN2 = float(np.log(2.0))


def iota(shape, dim):
    return lax.broadcasted_iota(jnp.int32, shape, dim)


def log2(n):
    return int(n).bit_length() - 1


def mm(a, b):
    return lax.dot_general(
        a, b, (((1,), (0,)), ((), ())),
        precision=lax.Precision.HIGHEST, preferred_element_type=jnp.float32,
    )


def pick(shape, test, value):
    return jnp.where(test(iota(shape, 0), iota(shape, 1)), jnp.float32(value), jnp.float32(0.0))


def left_coarse(rows, z):
    lz = log2(z)

    def test(i, j):
        return ((i >> (lz - 1)) == (j >> (lz + 1))) & (
            (i & (z // 2 - 1)) == ((j & (z - 1)) >> 1)
        )

    return pick((rows // 4, rows), test, 0.25)


def left_fine(rows, z):
    lz = log2(z)

    def test(j, i):
        return ((i >> (lz - 1)) == (j >> (lz + 1))) & (
            (i & (z // 2 - 1)) == ((j & (z - 1)) >> 1)
        )

    return pick((rows, rows // 4), test, 1.0)


def right_coarse(y):
    return pick((y, y // 2), lambda i, j: (i >> 1) == j, 0.5)


def right_fine(y):
    return pick((y // 2, y), lambda i, j: i == (j >> 1), 1.0)


def coarse2(v, z):
    return mm(mm(left_coarse(v.shape[0], z), v), right_coarse(v.shape[1]))


def fine2(v, z):
    return mm(mm(left_fine(v.shape[0] * 4, z), v), right_fine(v.shape[1] * 2))


def neighbours(v, z, xlo, xhi, edge):
    rows, y = v.shape
    row, lane = iota(v.shape, 0), iota(v.shape, 1)
    if xlo is None:
        xm = jnp.where(row < z, 0.0, pltpu.roll(v, z, 0))
        xp = jnp.where(row >= rows - z, 0.0, pltpu.roll(v, rows - z, 0))
        edge = jnp.zeros_like(v)
    else:
        xm = jnp.concatenate([xlo, v[: rows - z]], axis=0)
        xp = jnp.concatenate([v[z:], xhi], axis=0)
    zrow = row & (z - 1)
    zm = jnp.where(zrow == 0, 0.0, pltpu.roll(v, 1, 0))
    zp = jnp.where(zrow == z - 1, 0.0, pltpu.roll(v, rows - 1, 0))
    ym = jnp.where(lane == 0, edge, pltpu.roll(v, 1, 1))
    yp = jnp.where(lane == y - 1, edge, pltpu.roll(v, y - 1, 1))
    return xm, xp, zm, zp, ym, yp


def put_weights(w_ref, d, z, halo, scaling):
    total = None
    for i, other in enumerate(neighbours(d, z, *halo)):
        w = (0.5 * scaling) * (d + other)
        w_ref[i] = w
        total = w if total is None else total + w
    return total


def laplace(w_ref, v, z, halo):
    total = None
    for i, other in enumerate(neighbours(v, z, *halo)):
        term = w_ref[i] * (v - other)
        total = term if total is None else total + term
    return total


NO_HALO = (None, None, None)


def sinh_cosh(p):
    a, b = jnp.exp(p - LN2), jnp.exp(-p - LN2)
    q = jnp.minimum(p * p, 1.0)
    small = p * (
        1.0
        + q * (1 / 6) * (1.0 + q * (1 / 20) * (1.0 + q * (1 / 42) * (1.0 + q * (1 / 72) * (1.0 + q * (1 / 110)))))
    )
    return jnp.where(jnp.abs(p) < 1.0, small, a - b), a + b


def solver(
    slabs, bulks, nz, cx, y,
    d_in, rb_in, src_in, pot_ref, mis_ref,
    w0, w1, w2, w3, v2_ref,
    sx0, hx0, sy0, hy0, sx1, hx1, sy1, hy1,
    own, buf1, buf2,
    send_sem, recv_sem, s1_send, s1_recv, s2_send, s2_recv,
):
    s, b = lax.axis_index("slab"), lax.axis_index("bulk")
    z0, z1, z2, z3 = nz, nz // 2, nz // 4, nz // 8
    rows0, rows1 = cx * z0, (cx // 2) * z1
    r2 = (cx // 4) * z2
    y1 = y // 2
    y2 = y // 4
    for ref in (hx0, hy0, hx1, hy1):
        ref[...] = jnp.zeros_like(ref)

    barrier = pltpu.get_barrier_semaphore()
    for k in range(1, slabs):
        pl.semaphore_signal(
            barrier, inc=1, device_id=(lax.rem(s + k, slabs), b), device_id_type=MESH_ID
        )
    for k in range(1, bulks):
        pl.semaphore_signal(
            barrier, inc=1, device_id=(s, lax.rem(b + k, bulks)), device_id_type=MESH_ID
        )
    pl.semaphore_wait(barrier, slabs + bulks - 2)

    def halo_copies(level, phase):
        sx, hx, sy, hy = (sx0, hx0, sy0, hy0) if level == 0 else (sx1, hx1, sy1, hy1)
        slot = phase if level == 0 else 7 + phase
        made = []
        for side, (src, dst, to, can_send, can_recv) in enumerate((
            (sx.at[phase, 0], hx.at[phase, 0], (s, b + 1), b < bulks - 1, b > 0),
            (sx.at[phase, 1], hx.at[phase, 1], (s, b - 1), b > 0, b < bulks - 1),
            (sy.at[phase, 0], hy.at[phase, 0], (s + 1, b), s < slabs - 1, s > 0),
            (sy.at[phase, 1], hy.at[phase, 1], (s - 1, b), s > 0, s < slabs - 1),
        )):
            copy = pltpu.make_async_remote_copy(
                src_ref=src, dst_ref=dst,
                send_sem=send_sem.at[slot, side], recv_sem=recv_sem.at[slot, side],
                device_id=to, device_id_type=MESH_ID,
            )
            made.append((copy, can_send, can_recv))
        return made

    def start(level, phase, v):
        sx, sy = (sx0, sy0) if level == 0 else (sx1, sy1)
        z = z0 if level == 0 else z1
        rows, ys = v.shape
        sx[phase, 0] = v[rows - z :]
        sx[phase, 1] = v[:z]
        lane = iota((8, 128), 1)
        for side, at in ((0, ys - 1), (1, 0)):
            packed = jnp.zeros((8, 128), jnp.float32)
            for k in range(rows // 8):
                column = jnp.broadcast_to(v[8 * k : 8 * k + 8, at : at + 1], (8, 128))
                packed = jnp.where(lane == k, column, packed)
            sy[phase, side] = packed
        for copy, can_send, _ in halo_copies(level, phase):
            pl.when(can_send)(copy.start)

    def finish(level, phase):
        hx, hy = (hx0, hy0) if level == 0 else (hx1, hy1)
        rows, ys = (rows0, y) if level == 0 else (rows1, y1)
        for copy, _, can_recv in halo_copies(level, phase):
            pl.when(can_recv)(copy.wait_recv)
        low, high = hy[phase, 0], hy[phase, 1]
        lane = iota((8, ys), 1)
        tiles = []
        for k in range(rows // 8):
            tiles.append(jnp.where(
                lane == 0,
                jnp.broadcast_to(low[:, k : k + 1], (8, ys)),
                jnp.broadcast_to(high[:, k : k + 1], (8, ys)),
            ))
        return hx[phase, 0], hx[phase, 1], jnp.concatenate(tiles, axis=0)

    def exchange(level, phase, v):
        start(level, phase, v)
        return finish(level, phase)

    def gather_copies(n, stage):
        made = []
        size, me = (slabs, s) if stage == 0 else (bulks, b)
        for k in range(1, size):
            to = lax.rem(me + k, size)
            came = lax.rem(me + size - k, size)
            if stage == 0:
                make = lambda slot: pltpu.make_async_remote_copy(
                    src_ref=own.at[n], dst_ref=buf1.at[n, slot],
                    send_sem=s1_send.at[n, k], recv_sem=s1_recv.at[n, k],
                    device_id=(to, b), device_id_type=MESH_ID,
                )
            else:
                make = lambda slot: pltpu.make_async_remote_copy(
                    src_ref=buf1.at[n], dst_ref=buf2.at[n, slot],
                    send_sem=s2_send.at[n, k], recv_sem=s2_recv.at[n, k],
                    device_id=(s, to), device_id_type=MESH_ID,
                )
            made.append((make(me), make(came)))
        return made

    def gather(n, message):
        own[n] = message
        for out, _ in gather_copies(n, 0):
            out.start()
        buf1[n, s] = message
        for _, into in gather_copies(n, 0):
            into.wait_recv()
        for out, _ in gather_copies(n, 1):
            out.start()
        buf2[n, b] = buf1[n]
        for _, into in gather_copies(n, 1):
            into.wait_recv()

    def take(n, first, half):
        lane = iota((bulks * r2, 128), 1)
        tiles = []
        for t in range(slabs // 2):
            lo = buf2[n, :, 2 * t, first : first + r2, :].reshape(bulks * r2, 128)
            hi = buf2[n, :, 2 * t + 1, first : first + r2, :].reshape(bulks * r2, 128)
            if half == 0:
                hi = pltpu.roll(hi, 64, 1)
            else:
                lo = pltpu.roll(lo, 64, 1)
            tiles.append(jnp.where(lane < 64, lo, hi))
        return jnp.concatenate(tiles, axis=1)

    left12 = left_coarse(rows1, z1)
    right12a = pick((y1, 128), lambda i, j: (i >> 1) == j, 0.5)
    right12b = pick((y1, 128), lambda i, j: (i >> 1) + 64 == j, 0.5)

    d0 = d_in[...]
    start(0, 0, d0)
    d1 = coarse2(d0, z0)
    start(1, 0, d1)
    face0 = put_weights(w0, d0, z0, finish(0, 0), 1.0)
    face1 = put_weights(w1, d1, z1, finish(1, 0), 0.25)
    face2 = face3 = None
    rb = rb_in[...]
    src = src_in[...]
    pot = None
    for n in range(NEWTON):
        if n == 0:
            target, c0 = src, rb
        else:
            sh, ch = sinh_cosh(pot)
            target = src - laplace(w0, pot, z0, exchange(0, 3 * n, pot)) - rb * sh
            c0 = rb * ch
        step0 = damping / (face0 + c0)
        v0 = step0 * target
        start(0, 3 * n + 1, v0)
        c1 = coarse2(c0, z0)
        step1 = damping / (face1 + c1)
        res0 = target - laplace(w0, v0, z0, finish(0, 3 * n + 1)) - c0 * v0
        t1 = coarse2(res0, z0)
        v1 = step1 * t1
        start(1, n + 1, v1)
        xlo1, xhi1, edge1 = finish(1, n + 1)
        res1 = t1 - laplace(w1, v1, z1, (xlo1, xhi1, edge1)) - c1 * v1
        message = mm(left12, mm(res1, right12a) + mm(c1, right12b))
        if n == 0:
            extra = mm(left12, mm(d1, right12a))
        else:
            extra = jnp.zeros_like(message)
        gather(n, jnp.concatenate([message, extra], axis=0))
        t2, c2 = take(n, 0, 0), take(n, 0, 1)
        if n == 0:
            d2 = take(n, r2, 0)
            d3 = coarse2(d2, z2)
            face2 = put_weights(w2, d2, z2, NO_HALO, 0.25**2)
            face3 = put_weights(w3, d3, z3, NO_HALO, 0.25**3)
        step2 = damping / (face2 + c2)
        v2 = step2 * t2
        res2 = t2 - laplace(w2, v2, z2, NO_HALO) - c2 * v2
        t3, c3 = coarse2(res2, z2), coarse2(c2, z2)
        step3 = damping / (face3 + c3)
        v3 = step3 * t3
        for repeat in range(COARSE - 1):
            v3 = v3 + step3 * (t3 - laplace(w3, v3, z3, NO_HALO) - c3 * v3)
        v2 = v2 + fine2(v3, z2)
        v2 = v2 + step2 * (t2 - laplace(w2, v2, z2, NO_HALO) - c2 * v2)
        v2_ref[0:r2] = jnp.zeros((r2, slabs * y2), jnp.float32)
        v2_ref[r2 : r2 + bulks * r2] = v2
        v2_ref[r2 + bulks * r2 :] = jnp.zeros((r2, slabs * y2), jnp.float32)
        near = v2_ref[pl.ds(pl.multiple_of(b * r2, 8), 3 * r2), :]
        mine = pick((slabs * y2, y1), lambda i, j: i == (j >> 1) + s * y2, 1.0)
        rims = pick(
            (slabs * y2, y1),
            lambda i, j: ((j == 0) & (i == s * y2 - 1)) | ((j == y1 - 1) & (i == s * y2 + y2)),
            1.0,
        )
        near_mine = mm(near, mine)
        up = left_fine(rows1, z1)
        v1 = v1 + mm(up, near_mine[r2 : 2 * r2])
        xlo1 = xlo1 + mm(up, near_mine[0:r2])[rows1 - z1 :]
        xhi1 = xhi1 + mm(up, near_mine[2 * r2 :])[:z1]
        edge1 = edge1 + mm(up, mm(near[r2 : 2 * r2], rims))
        v1 = v1 + step1 * (t1 - laplace(w1, v1, z1, (xlo1, xhi1, edge1)) - c1 * v1)
        v0 = v0 + fine2(v1, z0)
        halo = exchange(0, 3 * n + 2, v0)
        v0 = v0 + step0 * (target - laplace(w0, v0, z0, halo) - c0 * v0)
        pot = v0 if n == 0 else pot + v0
    pot_ref[...] = pot
    sh, _ = sinh_cosh(pot)
    mis_ref[...] = laplace(w0, pot, z0, exchange(0, 3 * NEWTON, pot)) + rb * sh - src

    for level, count in ((0, 7), (1, 3)):
        for phase in range(count):
            for copy, can_send, _ in halo_copies(level, phase):
                pl.when(can_send)(copy.wait_send)
    for n in range(NEWTON):
        for stage in range(2):
            for out, _ in gather_copies(n, stage):
                out.wait_send()


def per_device(atom_counts, ion_flags, charge_cells, charge_values):
    slabs, bulks = lax.axis_size("slab"), lax.axis_size("bulk")
    density = atom_counts.astype(jnp.float32)
    along_y = taper_sum(jnp.pad(density, ((0, 0), (0, 0), (4, 4))), 2)
    extended = padded_2(along_y, (("slab", 0), ("bulk", 1)), 4)
    slab_shading = jnp.exp(-taper_sum(taper_sum(extended, 0), 1) / density_scale)
    shading = lax.all_to_all(slab_shading, "slab", split_axis=2, concat_axis=0, tiled=True)
    dielectric = 2.0 + 78.0 * shading
    access = shading * shading
    reaction_base = screening * access * (1.0 - ion_flags.astype(jnp.float32))
    flat_source = jnp.zeros((dielectric.size,), jnp.float32).at[charge_cells].add(charge_values)
    source = flat_source.reshape(dielectric.shape)

    nz, cx, y = dielectric.shape
    rows = nz * cx
    rows2 = (cx // 4) * (nz // 4)

    def flat(a):
        return a.transpose(1, 0, 2).reshape(rows, y)

    def back(a):
        return a.reshape(cx, nz, y).transpose(1, 0, 2)

    f32 = jnp.float32
    whole2 = (bulks * rows2, slabs * (y // 4))
    vm = pltpu.VMEM
    pot, mis = pl.pallas_call(
        lambda *refs: solver(slabs, bulks, nz, cx, y, *refs),
        out_shape=[jax.ShapeDtypeStruct((rows, y), f32)] * 2,
        in_specs=[pl.BlockSpec(memory_space=pltpu.VMEM)] * 3,
        out_specs=[pl.BlockSpec(memory_space=pltpu.VMEM)] * 2,
        scratch_shapes=[
            vm((6, rows, y), f32),
            vm((6, rows // 4, y // 2), f32),
            vm((6,) + whole2, f32),
            vm((6, whole2[0] // 4, whole2[1] // 2), f32),
            vm((whole2[0] + 2 * rows2, whole2[1]), f32),
            vm((7, 2, nz, y), f32), vm((7, 2, nz, y), f32),
            vm((7, 2, 8, 128), f32), vm((7, 2, 8, 128), f32),
            vm((3, 2, nz // 2, y // 2), f32), vm((3, 2, nz // 2, y // 2), f32),
            vm((3, 2, 8, 128), f32), vm((3, 2, 8, 128), f32),
            vm((2, 2 * rows2, 128), f32),
            vm((2, slabs, 2 * rows2, 128), f32),
            vm((2, bulks, slabs, 2 * rows2, 128), f32),
            pltpu.SemaphoreType.DMA((10, 4)), pltpu.SemaphoreType.DMA((10, 4)),
            pltpu.SemaphoreType.DMA((2, slabs)), pltpu.SemaphoreType.DMA((2, slabs)),
            pltpu.SemaphoreType.DMA((2, bulks)), pltpu.SemaphoreType.DMA((2, bulks)),
        ],
        compiler_params=pltpu.CompilerParams(
            collective_id=0, has_side_effects=True, vmem_limit_bytes=40 << 20
        ),
    )(flat(dielectric), flat(reaction_base), flat(source))
    return back(pot), back(mis)


def solution(mesh):
    placed = (
        P("slab", "bulk", None),
        P(None, "bulk", "slab"),
        P(("slab", "bulk")),
        P(("slab", "bulk")),
    )
    return jax.shard_map(
        per_device,
        mesh=mesh,
        in_specs=placed,
        out_specs=(P(None, "bulk", "slab"), P(None, "bulk", "slab")),
        check_vma=False,
    )
```

time: 588 us -> 109 us (0.19); the launches traced: 577 us -> 108 us
  blocking collectives: 197 us -> 0 us
  starting transfers between devices: 167 us -> 12.7 us
  waiting for transfers between devices: 100 us -> 9.26 us
  Pallas kernels: 0 us -> 60.4 us
  local copies, waits for them, and re-layouts: 68.2 us -> 12.6 us
  other arithmetic: 42.9 us -> 12.7 us
    all_gather x5 -> x0, blocking collectives: 197 us -> none  [the longest x2 81 us: multigrid(): lax.all_gather(reaction[None], ('slab', 'bulk'), axis=0, tiled=True)]
    ppermute x36 -> x2, starting transfers between devices: 104 us -> 6.24 us  [padded_2(): lax.ppermute(lax.slice_in_dim(block, block.shape[dim] - width, None, axis...]
    ppermute x36 -> x2, waiting for transfers between devices: 92.5 us -> 7.82 us  [padded_2(): lax.ppermute(lax.slice_in_dim(block, 0, width, axis=dim), axis, backward)]
    pallas_call x0 -> x1, Pallas kernels: none -> 60.4 us  [per_device(): pl.pallas_call(lambda *refs: solver(slabs, bulks, nz, cx, y, *refs), out_...]
    ppermute x36 -> x2, starting transfers between devices: 56.6 us -> 2.58 us  [padded_2(): lax.ppermute(lax.slice_in_dim(block, 0, width, axis=dim), axis, backward)]
    reshape x24 -> x0, local copies, waits for them, and re-layouts: 43.1 us -> none  [the longest x6 41.2 us: coarsen(): values_in.reshape(sizes_in[0] // 2, 2, sizes_in[1] // 2, 2, sizes_in[2] /...]
    reduce_sum x18 -> x0, other arithmetic: 21.6 us -> none  [coarsen(): return blocks.sum(axis=(1, 3, 5)) * 0.125]
    add x3 -> x2, local copies, waits for them, and re-layouts: 9.89 us -> 0.83 us  [per_device(): dielectric = 2.0 + 78.0 * shading]
  transfers between devices with their start and end apart: 73 -> 5, of which waited for: 37 -> 3; matrix products, arithmetic and copies ran while one was open for 9% -> 6% of each run, Pallas kernels for 0% -> 0%
where the time goes in v1:
time: 109 us; the launch traced here: 108 us
  Pallas kernels  60.4 us (55%)
  other arithmetic  12.7 us (12%)
  starting transfers between devices  12.7 us (12%)
  local copies, waits for them, and re-layouts  12.6 us (12%)
  waiting for transfers between devices  9.26 us (8%)
    pallas_call x1, Pallas kernels, per_device(): pl.pallas_call(lambda *refs: solver(slabs, bulks, nz, cx, y, *refs), out_...  60.4 us
    ppermute x2, waiting for transfers between devices, padded_2(): lax.ppermute(lax.slice_in_dim(block, 0, width, axis=dim), axis, backward)  7.82 us
    unnamed x8, local copies, waits for them, and re-layouts  7.21 us
    scatter-add x1, other arithmetic, per_device(): jnp.zeros((dielectric.size,), jnp.float32).at[charge_cells]  6.3 us
    ppermute x2, starting transfers between devices, padded_2(): lax.ppermute(lax.slice_in_dim(block, block.shape[dim] - width, None, axis...  6.24 us
    all_to_all x1, starting transfers between devices, per_device(): lax.all_to_all(slab_shading, 'slab', split_axis=2, concat_axis=0, tiled=T...  3.85 us
    add x1, other arithmetic, per_device(): dielectric = 2.0 + 78.0 * shading  3.66 us
    ppermute x2, starting transfers between devices, padded_2(): lax.ppermute(lax.slice_in_dim(block, 0, width, axis=dim), axis, backward)  2.58 us
  transfers between devices with their start and end apart: 5, of which 3 were waited for; matrix products, arithmetic and copies ran while one was open for 6% of the time, Pallas kernels for 0%

profile of v1, /device:TPU:0, one launch (start us, length us, event | category | flops | bytes accessed | tf_op | source)
XLA Modules:
  0.0 108.5 jit_solution(16824148071741960665)
XLA Ops:
  0.6 0.9 convert_element_type.8
  1.5 0.3 fusion.16
  1.9 4.9 %collective-permute-start = (f32[4,8,1024]{2,1,0:T(8,128)S(1)}, f32[4,8,1024]{2,1,0:T(8,128)S(1)}, u32[]{:S(2)}, u32[]{:S(2)}) collective-permute-start(f32[4,8,1024]{2,1,0:T(8,128)S(1)} %fusion.16), channel_id=1, source_target_pairs={{0,8},{8,16},{16,24},{1,9},{9,17},{17,25},{2,10},{10,18},{18,26},{... | collective-permute-start | bytes 393224 | tf_op jit(solution)/shard_map/ppermute | solution.py:26
  6.8 1.3 %collective-permute-start.1 = (f32[4,8,1024]{2,1,0:T(8,128)S(1)}, f32[4,8,1024]{2,1,0:T(8,128)S(1)}, u32[]{:S(2)}, u32[]{:S(2)}) collective-permute-start(f32[4,8,1024]{2,1,0:T(8,128)S(1)} %fusion.16), channel_id=1, source_target_pairs={{8,0},{16,8},{24,16},{9,1},{17,9},{25,17},{10,2},{18,10},{26,18},{... | collective-permute-start | bytes 393224 | tf_op jit(solution)/shard_map/ppermute | solution.py:29
  8.1 1.4 %collective-permute-done = f32[4,8,1024]{2,1,0:T(8,128)S(1)} collective-permute-done((f32[4,8,1024]{2,1,0:T(8,128)S(1)}, f32[4,8,1024]{2,1,0:T(8,128)S(1)}, u32[]{:S(2)}, u32[]{:S(2)}) %collective-permute-start) | collective-permute-done | bytes 131104 | tf_op jit(solution)/shard_map/ppermute | solution.py:26
  9.6 4.1 %collective-permute-done.1 = f32[4,8,1024]{2,1,0:T(8,128)S(1)} collective-permute-done((f32[4,8,1024]{2,1,0:T(8,128)S(1)}, f32[4,8,1024]{2,1,0:T(8,128)S(1)}, u32[]{:S(2)}, u32[]{:S(2)}) %collective-permute-start.1) | collective-permute-done | bytes 131104 | tf_op jit(solution)/shard_map/ppermute | solution.py:29
  13.7 0.1 fusion.37
  13.8 0.1 copy.35
  13.9 1.3 %collective-permute-start.2 = (f32[12,4,1024]{2,0,1:T(8,128)S(1)}, f32[12,4,1024]{2,0,1:T(8,128)S(1)}, u32[]{:S(2)}, u32[]{:S(2)}) collective-permute-start(f32[12,4,1024]{2,0,1:T(8,128)S(1)} %copy.35), channel_id=1, source_target_pairs={{0,1},{1,2},{2,3},{3,4},{4,5},{5,6},{6,7},{8,9},{9,10},{10,11},{11... | collective-permute-start | bytes 589832 | tf_op jit(solution)/shard_map/ppermute | solution.py:26
  15.3 0.1 copy.36
  15.4 1.3 %collective-permute-start.3 = (f32[12,4,1024]{2,0,1:T(8,128)S(1)}, f32[12,4,1024]{2,0,1:T(8,128)S(1)}, u32[]{:S(2)}, u32[]{:S(2)}) collective-permute-start(f32[12,4,1024]{2,0,1:T(8,128)S(1)} %copy.36), channel_id=1, source_target_pairs={{1,0},{2,1},{3,2},{4,3},{5,4},{6,5},{7,6},{9,8},{10,9},{11,10},{12... | collective-permute-start | bytes 589832 | tf_op jit(solution)/shard_map/ppermute | solution.py:29
  16.7 0.0 collective-permute-done.2
  16.7 0.1 copy.26
  16.8 3.7 %collective-permute-done.3 = f32[12,4,1024]{2,0,1:T(8,128)S(1)} collective-permute-done((f32[12,4,1024]{2,0,1:T(8,128)S(1)}, f32[12,4,1024]{2,0,1:T(8,128)S(1)}, u32[]{:S(2)}, u32[]{:S(2)}) %collective-permute-start.3) | collective-permute-done | bytes 196640 | tf_op jit(solution)/shard_map/ppermute | solution.py:29
  20.5 0.1 copy.27
  20.7 0.1 pad_maximum_fusion
  20.8 0.2 fusion
  21.0 0.2 fusion.27
  21.1 0.0 copy-start.1
  21.1 0.8 copy.28
  22.0 3.1 %reshape.49 = f32[4,1,8192]{2,1,0:T(1,128)} reshape(f32[1024,4,8]{2,1,0:T(4,128)S(1)} %bitcast.33) | data formatting | bytes 262144
  25.1 3.9 %all-to-all-start = ((f32[4,1,8192]{2,1,0:T(1,128)}), f32[4,1,8192]{2,1,0:T(1,128)S(1)}, u32[]{:S(2)}, u32[]{:S(2)}) async-start(f32[4,1,8192]{2,1,0:T(1,128)} %reshape.49), calls=%async_computation | async-start | bytes 262144 | tf_op jit(solution)/shard_map/all_to_all | solution.py:377
  28.9 0.0 copy-done.1
  28.9 6.3 %scatter_custom_fusion = f32[32768]{0:T(1024)S(1)} fusion(s32[1024]{0:T(1024)S(1)} %compare_select_fusion, f32[1024]{0:T(1024)} %param.7, f32[]{:T(128)} %constant.12.clone.1), kind=kCustom, calls=%fused_computation.68 | custom fusion | flops 1024 | bytes 131584 | tf_op jit(solution)/shard_map/scatter-add | solution.py:381
  35.3 0.0 all-to-all-done
  35.3 0.5 broadcast.65
  35.9 1.0 reduce
  36.8 3.9 %reshape.50 = f32[1024,4,8]{2,1,0:T(4,128)} reshape(f32[4,8192]{1,0:T(4,128)S(1)} %reduce) | data formatting | bytes 262144
  40.7 3.7 %multiply_add_fusion = (f32[4,8,1024]{1,0,2:T(4,128)S(1)}, f32[4,8,1024]{1,0,2:T(4,128)}) fusion(f32[1024,4,8]{2,1,0:T(4,128)} %reshape.50), kind=kLoop, calls=%fused_computation.1 | loop fusion | flops 98304 | bytes 393216 | tf_op jit(solution)/shard_map/add | solution.py:378
  44.4 0.0 copy-start
  44.4 1.9 %copy.30 = f32[4,4,8,256]{3,2,1,0:T(8,128)S(1)} copy(f32[4,4,8,256]{2,1,3,0:T(4,128)} %bitcast.32) | data formatting | bytes 262144 | tf_op jit(solution)/shard_map/mul | solution.py:379
  46.3 0.0 copy-done
  46.3 0.8 copy.29
  47.1 0.1 add.125
  47.2 60.4 %shard_map.59 = (f32[128,256]{1,0:T(8,128)S(1)}, f32[128,256]{1,0:T(8,128)S(1)}) custom-call(f32[128,256]{1,0:T(8,128)S(1)} %bitcast.28, f32[128,256]{1,0:T(8,128)S(1)} %bitcast.27, f32[128,256]{1,0:T(8,128)S(1)} %bitcast.26), custom_call_target="tpu_custom_call" | custom-call | tf_op jit(solution)/shard_map/pallas_call | solution.py:397
  107.6 0.9 copy_bitcast_fusion
  (6 shorter events, 0.2 us)
Async XLA Ops:
  1.9 7.7 %collective-permute-start = (f32[4,8,1024]{2,1,0:T(8,128)S(1)}, f32[4,8,1024]{2,1,0:T(8,128)S(1)}, u32[]{:S(2)}, u32[]{:S(2)}) collective-permute-start(f32[4,8,1024]{2,1,0:T(8,128)S(1)} %fusion.16), channel_id=1, source_target_pairs={{0,8},{8,16},{16,24},{1,9},{9,17},{17,25},{2,10},{10,18},{18,26},{... | collective-permute-start | bytes 393224 | tf_op jit(solution)/shard_map/ppermute | solution.py:26
  6.8 6.9 %collective-permute-start.1 = (f32[4,8,1024]{2,1,0:T(8,128)S(1)}, f32[4,8,1024]{2,1,0:T(8,128)S(1)}, u32[]{:S(2)}, u32[]{:S(2)}) collective-permute-start(f32[4,8,1024]{2,1,0:T(8,128)S(1)} %fusion.16), channel_id=1, source_target_pairs={{8,0},{16,8},{24,16},{9,1},{17,9},{25,17},{10,2},{18,10},{26,18},{... | collective-permute-start | bytes 393224 | tf_op jit(solution)/shard_map/ppermute | solution.py:29
  13.9 2.7 %collective-permute-start.2 = (f32[12,4,1024]{2,0,1:T(8,128)S(1)}, f32[12,4,1024]{2,0,1:T(8,128)S(1)}, u32[]{:S(2)}, u32[]{:S(2)}) collective-permute-start(f32[12,4,1024]{2,0,1:T(8,128)S(1)} %copy.35), channel_id=1, source_target_pairs={{0,1},{1,2},{2,3},{3,4},{4,5},{5,6},{6,7},{8,9},{9,10},{10,11},{11... | collective-permute-start | bytes 589832 | tf_op jit(solution)/shard_map/ppermute | solution.py:26
  15.4 5.1 %collective-permute-start.3 = (f32[12,4,1024]{2,0,1:T(8,128)S(1)}, f32[12,4,1024]{2,0,1:T(8,128)S(1)}, u32[]{:S(2)}, u32[]{:S(2)}) collective-permute-start(f32[12,4,1024]{2,0,1:T(8,128)S(1)} %copy.36), channel_id=1, source_target_pairs={{1,0},{2,1},{3,2},{4,3},{5,4},{6,5},{7,6},{9,8},{10,9},{11,10},{12... | collective-permute-start | bytes 589832 | tf_op jit(solution)/shard_map/ppermute | solution.py:29
  21.1 7.8 %copy-start.1 = (s32[1024]{0:T(1024)S(1)}, s32[1024]{0:T(1024)}, u32[]{:S(2)}) copy-start(s32[1024]{0:T(1024)} %param.6) | copy-start | bytes 12292
  25.1 10.3 %all-to-all-start = ((f32[4,1,8192]{2,1,0:T(1,128)}), f32[4,1,8192]{2,1,0:T(1,128)S(1)}, u32[]{:S(2)}, u32[]{:S(2)}) async-start(f32[4,1,8192]{2,1,0:T(1,128)} %reshape.49), calls=%async_computation | async-start | bytes 262144 | tf_op jit(solution)/shard_map/all_to_all | solution.py:377
  44.4 1.9 %copy-start = (s32[16,8,256]{2,1,0:T(8,128)S(1)}, s32[16,8,256]{2,1,0:T(8,128)}, u32[]{:S(2)}) copy-start(s32[16,8,256]{2,1,0:T(8,128)} %param.5) | copy-start | bytes 393220

commit v2 on v1

--- a/solution.py
+++ b/solution.py
@@ -16,29 +16,6 @@
 damping = 0.8
 screening = 1.0
 density_scale = 2.0
-
-
-def padded_2(block, sides, width):
-    for axis, dim in sides:
-        count = lax.axis_size(axis)
-        forward = [(i, i + 1) for i in range(count - 1)]
-        backward = [(target, source) for source, target in forward]
-        low = lax.ppermute(
-            lax.slice_in_dim(block, block.shape[dim] - width, None, axis=dim), axis, forward
-        )
-        high = lax.ppermute(lax.slice_in_dim(block, 0, width, axis=dim), axis, backward)
-        block = jnp.concatenate([low, block, high], axis=dim)
-    return block
-
-
-def taper_sum(padded, dimension):
-    length = padded.shape[dimension] - 8
-    summed = float(taper_weights[0]) * lax.slice_in_dim(padded, 0, length, axis=dimension)
-    for offset in range(1, 9):
-        summed = summed + float(taper_weights[offset]) * lax.slice_in_dim(
-            padded, offset, offset + length, axis=dimension
-        )
-    return summed
 
 
 MESH_ID = pl.DeviceIdType.MESH
@@ -150,13 +127,47 @@
     return jnp.where(jnp.abs(p) < 1.0, small, a - b), a + b
 
 
+def taper_y(density):
+    width = density.shape[1]
+    lane = iota(density.shape, 1)
+    summed = float(taper_weights[4]) * density
+    for k in range(1, 5):
+        before = jnp.where(lane < k, 0.0, pltpu.roll(density, k, 1))
+        after = jnp.where(lane >= width - k, 0.0, pltpu.roll(density, width - k, 1))
+        summed = summed + float(taper_weights[4 + k]) * (before + after)
+    return summed
+
+
+def taper_z(rows, z, cx):
+    i, j = iota((rows, rows), 0), iota((rows, rows), 1)
+    far = jnp.abs((i & (z - 1)) - (j >> log2(cx)))
+    band = jnp.zeros((rows, rows), jnp.float32)
+    for k in range(5):
+        band = jnp.where(far == k, float(taper_weights[4 + k]), band)
+    return jnp.where((i >> log2(z)) == (j & (cx - 1)), band, 0.0)
+
+
+def scattered(cells, values, rows, z, cx, y):
+    entries = cells.shape[1]
+    ly, lx = log2(y), log2(cx)
+    row = ((cells >> ly) & (cx - 1)) * z + (cells >> (ly + lx))
+    at_row = jnp.where(iota((rows, entries), 0) == row, values, 0.0)
+    at_y = jnp.where(iota((y, entries), 0) == (cells & (y - 1)), jnp.float32(1.0), jnp.float32(0.0))
+    return lax.dot_general(
+        at_row, at_y, (((1,), (1,)), ((), ())),
+        precision=lax.Precision.HIGHEST, preferred_element_type=jnp.float32,
+    )
+
+
 def solver(
     slabs, bulks, nz, cx, y,
-    d_in, rb_in, src_in, pot_ref, mis_ref,
+    atoms_in, flags_in, cells_in, values_in, pot_ref, mis_ref,
+    ay, abuf, ty, hty,
     w0, w1, w2, w3, v2_ref,
     sx0, hx0, sy0, hy0, sx1, hx1, sy1, hy1,
     own, buf1, buf2,
     send_sem, recv_sem, s1_send, s1_recv, s2_send, s2_recv,
+    a_send, a_recv, t_send, t_recv,
 ):
     s, b = lax.axis_index("slab"), lax.axis_index("bulk")
     z0, z1, z2, z3 = nz, nz // 2, nz // 4, nz // 8
@@ -164,7 +175,7 @@
     r2 = (cx // 4) * z2
     y1 = y // 2
     y2 = y // 4
-    for ref in (hx0, hy0, hx1, hy1):
+    for ref in (hx0, hy0, hx1, hy1, hty):
         ref[...] = jnp.zeros_like(ref)
 
     barrier = pltpu.get_barrier_semaphore()
@@ -283,15 +294,62 @@
     right12a = pick((y1, 128), lambda i, j: (i >> 1) == j, 0.5)
     right12b = pick((y1, 128), lambda i, j: (i >> 1) + 64 == j, 0.5)
 
-    d0 = d_in[...]
+    density = atoms_in[...].astype(jnp.float32).reshape(-1, slabs * y)
+    smooth_y = taper_y(density)
+    for t in range(slabs):
+        ay[t] = smooth_y[:, t * y : (t + 1) * y]
+    slab_copies = []
+    for k in range(1, slabs):
+        to, came = lax.rem(s + k, slabs), lax.rem(s + slabs - k, slabs)
+        slab_copies.append([
+            pltpu.make_async_remote_copy(
+                src_ref=ay.at[to], dst_ref=abuf.at[slot],
+                send_sem=a_send.at[k], recv_sem=a_recv.at[k],
+                device_id=(to, b), device_id_type=MESH_ID,
+            )
+            for slot in (s, came)
+        ])
+    for out, _ in slab_copies:
+        out.start()
+    abuf[s] = ay[s]
+    src = scattered(cells_in[...], values_in[...], rows0, z0, cx, y)
+    to_x = pick((rows0, rows0), lambda i, j: (i >> log2(z0)) + ((i & (z0 - 1)) << log2(cx)) == j, 1.0)
+    open_cells = 1.0 - mm(to_x, flags_in[...].astype(jnp.float32).reshape(rows0, y))
+    along_z = taper_z(rows0, z0, cx)
+    for _, into in slab_copies:
+        into.wait_recv()
+    smooth_z = mm(along_z, abuf[...].reshape(rows0, y))
+    ty[0] = smooth_z[rows0 - 4 * z0 :]
+    ty[1] = smooth_z[: 4 * z0]
+    row_copies = []
+    for side, (to, can_send, can_recv) in enumerate((
+        ((s, b + 1), b < bulks - 1, b > 0),
+        ((s, b - 1), b > 0, b < bulks - 1),
+    )):
+        row_copies.append((
+            pltpu.make_async_remote_copy(
+                src_ref=ty.at[side], dst_ref=hty.at[side],
+                send_sem=t_send.at[side], recv_sem=t_recv.at[side],
+                device_id=to, device_id_type=MESH_ID,
+            ), can_send, can_recv,
+        ))
+    for copy, can_send, _ in row_copies:
+        pl.when(can_send)(copy.start)
+    for copy, _, can_recv in row_copies:
+        pl.when(can_recv)(copy.wait_recv)
+    extended = jnp.concatenate([hty[0], smooth_z, hty[1]], axis=0)
+    smoothed = float(taper_weights[0]) * extended[:rows0]
+    for k in range(1, 9):
+        smoothed = smoothed + float(taper_weights[k]) * extended[k * z0 : k * z0 + rows0]
+    shading = jnp.exp(-smoothed / density_scale)
+    d0 = 2.0 + 78.0 * shading
+    rb = screening * shading * shading * open_cells
     start(0, 0, d0)
     d1 = coarse2(d0, z0)
     start(1, 0, d1)
     face0 = put_weights(w0, d0, z0, finish(0, 0), 1.0)
     face1 = put_weights(w1, d1, z1, finish(1, 0), 0.25)
     face2 = face3 = None
-    rb = rb_in[...]
-    src = src_in[...]
     pot = None
     for n in range(NEWTON):
         if n == 0:
@@ -354,10 +412,17 @@
         halo = exchange(0, 3 * n + 2, v0)
         v0 = v0 + step0 * (target - laplace(w0, v0, z0, halo) - c0 * v0)
         pot = v0 if n == 0 else pot + v0
-    pot_ref[...] = pot
+    start(0, 3 * NEWTON, pot)
+    from_x = pick((rows0, rows0), lambda i, j: (j >> log2(z0)) + ((j & (z0 - 1)) << log2(cx)) == i, 1.0)
+    pot_ref[...] = mm(from_x, pot).reshape(nz, cx, y)
     sh, _ = sinh_cosh(pot)
-    mis_ref[...] = laplace(w0, pot, z0, exchange(0, 3 * NEWTON, pot)) + rb * sh - src
-
+    misfit = laplace(w0, pot, z0, finish(0, 3 * NEWTON)) + rb * sh - src
+    mis_ref[...] = mm(from_x, misfit).reshape(nz, cx, y)
+
+    for out, _ in slab_copies:
+        out.wait_send()
+    for copy, can_send, _ in row_copies:
+        pl.when(can_send)(copy.wait_send)
     for level, count in ((0, 7), (1, 3)):
         for phase in range(count):
             for copy, can_send, _ in halo_copies(level, phase):
@@ -370,36 +435,20 @@
 
 def per_device(atom_counts, ion_flags, charge_cells, charge_values):
     slabs, bulks = lax.axis_size("slab"), lax.axis_size("bulk")
-    density = atom_counts.astype(jnp.float32)
-    along_y = taper_sum(jnp.pad(density, ((0, 0), (0, 0), (4, 4))), 2)
-    extended = padded_2(along_y, (("slab", 0), ("bulk", 1)), 4)
-    slab_shading = jnp.exp(-taper_sum(taper_sum(extended, 0), 1) / density_scale)
-    shading = lax.all_to_all(slab_shading, "slab", split_axis=2, concat_axis=0, tiled=True)
-    dielectric = 2.0 + 78.0 * shading
-    access = shading * shading
-    reaction_base = screening * access * (1.0 - ion_flags.astype(jnp.float32))
-    flat_source = jnp.zeros((dielectric.size,), jnp.float32).at[charge_cells].add(charge_values)
-    source = flat_source.reshape(dielectric.shape)
-
-    nz, cx, y = dielectric.shape
+    nz, cx, y = ion_flags.shape
     rows = nz * cx
     rows2 = (cx // 4) * (nz // 4)
-
-    def flat(a):
-        return a.transpose(1, 0, 2).reshape(rows, y)
-
-    def back(a):
-        return a.reshape(cx, nz, y).transpose(1, 0, 2)
-
     f32 = jnp.float32
     whole2 = (bulks * rows2, slabs * (y // 4))
     vm = pltpu.VMEM
     pot, mis = pl.pallas_call(
         lambda *refs: solver(slabs, bulks, nz, cx, y, *refs),
-        out_shape=[jax.ShapeDtypeStruct((rows, y), f32)] * 2,
-        in_specs=[pl.BlockSpec(memory_space=pltpu.VMEM)] * 3,
+        out_shape=[jax.ShapeDtypeStruct((nz, cx, y), f32)] * 2,
+        in_specs=[pl.BlockSpec(memory_space=pltpu.VMEM)] * 4,
         out_specs=[pl.BlockSpec(memory_space=pltpu.VMEM)] * 2,
         scratch_shapes=[
+            vm((slabs, rows // slabs, y), f32), vm((slabs, rows // slabs, y), f32),
+            vm((2, 4 * nz, y), f32), vm((2, 4 * nz, y), f32),
             vm((6, rows, y), f32),
             vm((6, rows // 4, y // 2), f32),
             vm((6,) + whole2, f32),
@@ -415,12 +464,14 @@
             pltpu.SemaphoreType.DMA((10, 4)), pltpu.SemaphoreType.DMA((10, 4)),
             pltpu.SemaphoreType.DMA((2, slabs)), pltpu.SemaphoreType.DMA((2, slabs)),
             pltpu.SemaphoreType.DMA((2, bulks)), pltpu.SemaphoreType.DMA((2, bulks)),
+            pltpu.SemaphoreType.DMA((slabs,)), pltpu.SemaphoreType.DMA((slabs,)),
+            pltpu.SemaphoreType.DMA((2,)), pltpu.SemaphoreType.DMA((2,)),
         ],
         compiler_params=pltpu.CompilerParams(
             collective_id=0, has_side_effects=True, vmem_limit_bytes=40 << 20
         ),
-    )(flat(dielectric), flat(reaction_base), flat(source))
-    return back(pot), back(mis)
+    )(atom_counts, ion_flags, charge_cells[None], charge_values[None])
+    return pot, mis
 
 
 def solution(mesh):

time: 109 us -> 71.3 us (0.65)
  other arithmetic: 12.7 us -> 0 us
  starting transfers between devices: 12.7 us -> 0 us
  waiting for transfers between devices: 9.26 us -> 0 us
  local copies, waits for them, and re-layouts: 12.6 us -> 4.49 us
  Pallas kernels: 60.4 us -> 66 us
    ppermute x4 -> x0, waiting for transfers between devices: 9.26 us -> none  [the longest x2 7.82 us: padded_2(): lax.ppermute(lax.slice_in_dim(block, 0, width, axis=dim), axis, backward)]
    ppermute x4 -> x0, starting transfers between devices: 8.83 us -> none  [the longest x2 6.24 us: padded_2(): lax.ppermute(lax.slice_in_dim(block, block.shape[dim] - width, None, axis...]
    scatter-add x1 -> x0, other arithmetic: 6.3 us -> none  [per_device(): jnp.zeros((dielectric.size,), jnp.float32).at[charge_cells]]
    pallas_call x1, Pallas kernels: 60.4 us -> 66 us  [per_device(): pl.pallas_call(lambda *refs: solver(slabs, bulks, nz, cx, y, *refs), out_...]
    add x3 -> x0, other arithmetic: 4.15 us -> none  [the longest x1 3.66 us: per_device(): dielectric = 2.0 + 78.0 * shading]
    all_to_all x1 -> x0, starting transfers between devices: 3.85 us -> none  [per_device(): lax.all_to_all(slab_shading, 'slab', split_axis=2, concat_axis=0, tiled=T...]
    unnamed x8 -> x10, local copies, waits for them, and re-layouts: 7.21 us -> 4.49 us
    mul x1 -> x0, local copies, waits for them, and re-layouts: 1.87 us -> none  [per_device(): access = shading * shading]
  transfers between devices with their start and end apart: 5 -> 0, of which waited for: 3 -> 0; matrix products, arithmetic and copies ran while one was open for 6% -> 0% of each run, Pallas kernels for 0% -> 0%
where the time goes in v2:
time: 71.3 us; the launch traced here: 71.1 us
  Pallas kernels  66 us (93%)
  local copies, waits for them, and re-layouts  4.49 us (6%)
    pallas_call x1, Pallas kernels, per_device(): pl.pallas_call(lambda *refs: solver(slabs, bulks, nz, cx, y, *refs), out_...  66 us
    unnamed x10, local copies, waits for them, and re-layouts  4.49 us

profile of v2, /device:TPU:0, one launch (start us, length us, event | category | flops | bytes accessed | tf_op | source)
XLA Modules:
  0.0 71.1 jit_solution(17625120767156110197)
XLA Ops:
  0.6 0.0 copy-start
  0.6 0.9 %copy-done = s32[4,8,1024]{2,1,0:T(8,128)S(1)} copy-done((s32[4,8,1024]{2,1,0:T(8,128)S(1)}, s32[4,8,1024]{2,1,0:T(8,128)}, u32[]{:S(2)}) %copy-start) | copy-done | bytes 131096
  1.5 0.0 copy-start.1
  1.5 0.9 %copy-done.1 = s32[16,8,256]{2,1,0:T(8,128)S(1)} copy-done((s32[16,8,256]{2,1,0:T(8,128)S(1)}, s32[16,8,256]{2,1,0:T(8,128)}, u32[]{:S(2)}) %copy-start.1) | copy-done | bytes 131096
  2.4 0.0 copy-start.2
  2.4 0.7 copy-done.2
  3.1 0.0 copy-start.3
  3.1 0.7 copy-done.3
  3.8 66.0 %shard_map.59 = (f32[16,8,256]{2,1,0:T(8,128)S(1)}, f32[16,8,256]{2,1,0:T(8,128)S(1)}) custom-call(s32[4,8,1024]{2,1,0:T(8,128)S(1)} %copy-done, s32[16,8,256]{2,1,0:T(8,128)S(1)} %copy-done.1, s32[1,1024]{1,0:T(1,128)S(1)} %bitcast.2, f32[1,1024]{1,0:T(1,128)S(1)} %bitcast.3), custom_call_target="tpu_custom_call" | custom-call | tf_op jit(solution)/shard_map/pallas_call | solution.py:444
  69.8 0.7 copy.8
  70.4 0.7 copy.9
Async XLA Ops:
  0.6 0.9 %copy-start = (s32[4,8,1024]{2,1,0:T(8,128)S(1)}, s32[4,8,1024]{2,1,0:T(8,128)}, u32[]{:S(2)}) copy-start(s32[4,8,1024]{2,1,0:T(8,128)} %refs_0_.1) | copy-start | bytes 393220
  1.5 0.9 %copy-start.1 = (s32[16,8,256]{2,1,0:T(8,128)S(1)}, s32[16,8,256]{2,1,0:T(8,128)}, u32[]{:S(2)}) copy-start(s32[16,8,256]{2,1,0:T(8,128)} %refs_1_.1) | copy-start | bytes 393220
  2.4 0.7 copy-start.2
  3.1 0.7 copy-start.3

commit v3 on v2

--- a/solution.py
+++ b/solution.py
@@ -19,6 +19,7 @@
 
 
 MESH_ID = pl.DeviceIdType.MESH
+GATHER_UNROLL = 1
 LN2 = float(np.log(2.0))
 
 
@@ -117,6 +118,16 @@
 NO_HALO = (None, None, None)
 
 
+def rim_part(w_ref, inner, z, halo):
+    xlo, xhi, edge = halo
+    rows, y = inner.shape
+    lane = iota(inner.shape, 1)
+    inner = inner - jnp.where(lane == 0, w_ref[4] * edge, jnp.where(lane == y - 1, w_ref[5] * edge, 0.0))
+    first = inner[:z] - w_ref[0, :z] * xlo
+    last = inner[rows - z :] - w_ref[1, rows - z :] * xhi
+    return jnp.concatenate([first, inner[z : rows - z], last], axis=0)
+
+
 def sinh_cosh(p):
     a, b = jnp.exp(p - LN2), jnp.exp(-p - LN2)
     q = jnp.minimum(p * p, 1.0)
@@ -161,13 +172,14 @@
 
 def solver(
     slabs, bulks, nz, cx, y,
-    atoms_in, flags_in, cells_in, values_in, pot_ref, mis_ref,
+    atoms_hbm, flags_hbm, cells_hbm, values_hbm, pot_ref, mis_ref,
+    atoms_in, flags_in, cells_in, values_in,
     ay, abuf, ty, hty,
     w0, w1, w2, w3, v2_ref,
     sx0, hx0, sy0, hy0, sx1, hx1, sy1, hy1,
     own, buf1, buf2,
     send_sem, recv_sem, s1_send, s1_recv, s2_send, s2_recv,
-    a_send, a_recv, t_send, t_recv,
+    a_send, a_recv, t_send, t_recv, load_sem,
 ):
     s, b = lax.axis_index("slab"), lax.axis_index("bulk")
     z0, z1, z2, z3 = nz, nz // 2, nz // 4, nz // 8
@@ -175,10 +187,22 @@
     r2 = (cx // 4) * z2
     y1 = y // 2
     y2 = y // 4
+    loads = [
+        pltpu.make_async_copy(there, here, load_sem.at[i])
+        for i, (there, here) in enumerate((
+            (atoms_hbm, atoms_in), (flags_hbm, flags_in),
+            (cells_hbm, cells_in), (values_hbm, values_in),
+        ))
+    ]
+    for load in loads:
+        load.start()
     for ref in (hx0, hy0, hx1, hy1, hty):
         ref[...] = jnp.zeros_like(ref)
 
+    count = slabs * bulks
+    me = s * bulks + b
     barrier = pltpu.get_barrier_semaphore()
+
     for k in range(1, slabs):
         pl.semaphore_signal(
             barrier, inc=1, device_id=(lax.rem(s + k, slabs), b), device_id_type=MESH_ID
@@ -187,7 +211,6 @@
         pl.semaphore_signal(
             barrier, inc=1, device_id=(s, lax.rem(b + k, bulks)), device_id_type=MESH_ID
         )
-    pl.semaphore_wait(barrier, slabs + bulks - 2)
 
     def halo_copies(level, phase):
         sx, hx, sy, hy = (sx0, hx0, sy0, hy0) if level == 0 else (sx1, hx1, sy1, hy1)
@@ -239,9 +262,10 @@
             ))
         return hx[phase, 0], hx[phase, 1], jnp.concatenate(tiles, axis=0)
 
-    def exchange(level, phase, v):
+    def around(level, phase, w_ref, v, z):
         start(level, phase, v)
-        return finish(level, phase)
+        inner = laplace(w_ref, v, z, NO_HALO)
+        return rim_part(w_ref, inner, z, finish(level, phase))
 
     def gather_copies(n, stage):
         made = []
@@ -264,25 +288,29 @@
             made.append((make(me), make(came)))
         return made
 
-    def gather(n, message):
+    def gather_begin(n, message):
         own[n] = message
         for out, _ in gather_copies(n, 0):
             out.start()
         buf1[n, s] = message
+
+    def gather_pass(n):
         for _, into in gather_copies(n, 0):
             into.wait_recv()
         for out, _ in gather_copies(n, 1):
             out.start()
         buf2[n, b] = buf1[n]
+
+    def gather_end(n):
         for _, into in gather_copies(n, 1):
             into.wait_recv()
 
-    def take(n, first, half):
+    def take(n, half):
         lane = iota((bulks * r2, 128), 1)
         tiles = []
         for t in range(slabs // 2):
-            lo = buf2[n, :, 2 * t, first : first + r2, :].reshape(bulks * r2, 128)
-            hi = buf2[n, :, 2 * t + 1, first : first + r2, :].reshape(bulks * r2, 128)
+            lo = buf2[n, :, 2 * t].reshape(bulks * r2, 128)
+            hi = buf2[n, :, 2 * t + 1].reshape(bulks * r2, 128)
             if half == 0:
                 hi = pltpu.roll(hi, 64, 1)
             else:
@@ -294,6 +322,7 @@
     right12a = pick((y1, 128), lambda i, j: (i >> 1) == j, 0.5)
     right12b = pick((y1, 128), lambda i, j: (i >> 1) + 64 == j, 0.5)
 
+    loads[0].wait()
     density = atoms_in[...].astype(jnp.float32).reshape(-1, slabs * y)
     smooth_y = taper_y(density)
     for t in range(slabs):
@@ -309,9 +338,12 @@
             )
             for slot in (s, came)
         ])
+    pl.semaphore_wait(barrier, slabs + bulks - 2)
     for out, _ in slab_copies:
         out.start()
     abuf[s] = ay[s]
+    for load in loads[1:]:
+        load.wait()
     src = scattered(cells_in[...], values_in[...], rows0, z0, cx, y)
     to_x = pick((rows0, rows0), lambda i, j: (i >> log2(z0)) + ((i & (z0 - 1)) << log2(cx)) == j, 1.0)
     open_cells = 1.0 - mm(to_x, flags_in[...].astype(jnp.float32).reshape(rows0, y))
@@ -347,8 +379,10 @@
     start(0, 0, d0)
     d1 = coarse2(d0, z0)
     start(1, 0, d1)
+    gather_begin(NEWTON, mm(left12, mm(d1, right12a)))
     face0 = put_weights(w0, d0, z0, finish(0, 0), 1.0)
     face1 = put_weights(w1, d1, z1, finish(1, 0), 0.25)
+    gather_pass(NEWTON)
     face2 = face3 = None
     pot = None
     for n in range(NEWTON):
@@ -356,28 +390,30 @@
             target, c0 = src, rb
         else:
             sh, ch = sinh_cosh(pot)
-            target = src - laplace(w0, pot, z0, exchange(0, 3 * n, pot)) - rb * sh
+            target = src - around(0, 3 * n, w0, pot, z0) - rb * sh
             c0 = rb * ch
         step0 = damping / (face0 + c0)
         v0 = step0 * target
         start(0, 3 * n + 1, v0)
         c1 = coarse2(c0, z0)
         step1 = damping / (face1 + c1)
-        res0 = target - laplace(w0, v0, z0, finish(0, 3 * n + 1)) - c0 * v0
+        inner0 = laplace(w0, v0, z0, NO_HALO)
+        res0 = target - rim_part(w0, inner0, z0, finish(0, 3 * n + 1)) - c0 * v0
         t1 = coarse2(res0, z0)
         v1 = step1 * t1
         start(1, n + 1, v1)
+        inner1 = laplace(w1, v1, z1, NO_HALO)
+        c1_part = mm(c1, right12b)
         xlo1, xhi1, edge1 = finish(1, n + 1)
-        res1 = t1 - laplace(w1, v1, z1, (xlo1, xhi1, edge1)) - c1 * v1
-        message = mm(left12, mm(res1, right12a) + mm(c1, right12b))
+        res1 = t1 - rim_part(w1, inner1, z1, (xlo1, xhi1, edge1)) - c1 * v1
+        message = mm(left12, mm(res1, right12a) + c1_part)
+        gather_begin(n, message)
+        gather_pass(n)
+        gather_end(n)
+        t2, c2 = take(n, 0), take(n, 1)
         if n == 0:
-            extra = mm(left12, mm(d1, right12a))
-        else:
-            extra = jnp.zeros_like(message)
-        gather(n, jnp.concatenate([message, extra], axis=0))
-        t2, c2 = take(n, 0, 0), take(n, 0, 1)
-        if n == 0:
-            d2 = take(n, r2, 0)
+            gather_end(NEWTON)
+            d2 = take(NEWTON, 0)
             d3 = coarse2(d2, z2)
             face2 = put_weights(w2, d2, z2, NO_HALO, 0.25**2)
             face3 = put_weights(w3, d3, z3, NO_HALO, 0.25**3)
@@ -409,14 +445,14 @@
         edge1 = edge1 + mm(up, mm(near[r2 : 2 * r2], rims))
         v1 = v1 + step1 * (t1 - laplace(w1, v1, z1, (xlo1, xhi1, edge1)) - c1 * v1)
         v0 = v0 + fine2(v1, z0)
-        halo = exchange(0, 3 * n + 2, v0)
-        v0 = v0 + step0 * (target - laplace(w0, v0, z0, halo) - c0 * v0)
+        v0 = v0 + step0 * (target - around(0, 3 * n + 2, w0, v0, z0) - c0 * v0)
         pot = v0 if n == 0 else pot + v0
     start(0, 3 * NEWTON, pot)
     from_x = pick((rows0, rows0), lambda i, j: (j >> log2(z0)) + ((j & (z0 - 1)) << log2(cx)) == i, 1.0)
     pot_ref[...] = mm(from_x, pot).reshape(nz, cx, y)
     sh, _ = sinh_cosh(pot)
-    misfit = laplace(w0, pot, z0, finish(0, 3 * NEWTON)) + rb * sh - src
+    inner = laplace(w0, pot, z0, NO_HALO) + rb * sh - src
+    misfit = rim_part(w0, inner, z0, finish(0, 3 * NEWTON))
     mis_ref[...] = mm(from_x, misfit).reshape(nz, cx, y)
 
     for out, _ in slab_copies:
@@ -427,7 +463,7 @@
         for phase in range(count):
             for copy, can_send, _ in halo_copies(level, phase):
                 pl.when(can_send)(copy.wait_send)
-    for n in range(NEWTON):
+    for n in range(NEWTON + 1):
         for stage in range(2):
             for out, _ in gather_copies(n, stage):
                 out.wait_send()
@@ -444,9 +480,11 @@
     pot, mis = pl.pallas_call(
         lambda *refs: solver(slabs, bulks, nz, cx, y, *refs),
         out_shape=[jax.ShapeDtypeStruct((nz, cx, y), f32)] * 2,
-        in_specs=[pl.BlockSpec(memory_space=pltpu.VMEM)] * 4,
+        in_specs=[pl.BlockSpec(memory_space=pl.ANY)] * 4,
         out_specs=[pl.BlockSpec(memory_space=pltpu.VMEM)] * 2,
         scratch_shapes=[
+            vm(atom_counts.shape, jnp.int32), vm(ion_flags.shape, jnp.int32),
+            vm((1,) + charge_cells.shape, jnp.int32), vm((1,) + charge_values.shape, f32),
             vm((slabs, rows // slabs, y), f32), vm((slabs, rows // slabs, y), f32),
             vm((2, 4 * nz, y), f32), vm((2, 4 * nz, y), f32),
             vm((6, rows, y), f32),
@@ -458,14 +496,15 @@
             vm((7, 2, 8, 128), f32), vm((7, 2, 8, 128), f32),
             vm((3, 2, nz // 2, y // 2), f32), vm((3, 2, nz // 2, y // 2), f32),
             vm((3, 2, 8, 128), f32), vm((3, 2, 8, 128), f32),
-            vm((2, 2 * rows2, 128), f32),
-            vm((2, slabs, 2 * rows2, 128), f32),
-            vm((2, bulks, slabs, 2 * rows2, 128), f32),
+            vm((NEWTON + 1, rows2, 128), f32),
+            vm((NEWTON + 1, slabs, rows2, 128), f32),
+            vm((NEWTON + 1, bulks, slabs, rows2, 128), f32),
             pltpu.SemaphoreType.DMA((10, 4)), pltpu.SemaphoreType.DMA((10, 4)),
-            pltpu.SemaphoreType.DMA((2, slabs)), pltpu.SemaphoreType.DMA((2, slabs)),
-            pltpu.SemaphoreType.DMA((2, bulks)), pltpu.SemaphoreType.DMA((2, bulks)),
+            pltpu.SemaphoreType.DMA((NEWTON + 1, slabs)), pltpu.SemaphoreType.DMA((NEWTON + 1, slabs)),
+            pltpu.SemaphoreType.DMA((NEWTON + 1, bulks)), pltpu.SemaphoreType.DMA((NEWTON + 1, bulks)),
             pltpu.SemaphoreType.DMA((slabs,)), pltpu.SemaphoreType.DMA((slabs,)),
             pltpu.SemaphoreType.DMA((2,)), pltpu.SemaphoreType.DMA((2,)),
+            pltpu.SemaphoreType.DMA((4,)),
         ],
         compiler_params=pltpu.CompilerParams(
             collective_id=0, has_side_effects=True, vmem_limit_bytes=40 << 20

time: 71.3 us -> 69.9 us (0.980)
  Pallas kernels: 66 us -> 64.5 us
    pallas_call x1, Pallas kernels: 66 us -> 64.5 us  [per_device(): pl.pallas_call(lambda *refs: solver(slabs, bulks, nz, cx, y, *refs), out_...]
where the time goes in v3:
time: 69.9 us; the launch traced here: 69.6 us
  Pallas kernels  64.5 us (92%)
  local copies, waits for them, and re-layouts  4.49 us (6%)
    pallas_call x1, Pallas kernels, per_device(): pl.pallas_call(lambda *refs: solver(slabs, bulks, nz, cx, y, *refs), out_...  64.5 us
    unnamed x10, local copies, waits for them, and re-layouts  4.49 us

profile of v3, /device:TPU:0, one launch (start us, length us, event | category | flops | bytes accessed | tf_op | source)
XLA Modules:
  0.0 69.6 jit_solution(705797430057166)
XLA Ops:
  0.6 0.0 copy-start
  0.6 0.9 %copy-done = s32[4,8,1024]{2,1,0:T(8,128)S(1)} copy-done((s32[4,8,1024]{2,1,0:T(8,128)S(1)}, s32[4,8,1024]{2,1,0:T(8,128)}, u32[]{:S(2)}) %copy-start) | copy-done | bytes 131096
  1.5 0.0 copy-start.1
  1.5 0.9 %copy-done.1 = s32[16,8,256]{2,1,0:T(8,128)S(1)} copy-done((s32[16,8,256]{2,1,0:T(8,128)S(1)}, s32[16,8,256]{2,1,0:T(8,128)}, u32[]{:S(2)}) %copy-start.1) | copy-done | bytes 131096
  2.4 0.0 copy-start.2
  2.4 0.7 copy-done.2
  3.1 0.0 copy-start.3
  3.1 0.7 copy-done.3
  3.8 64.5 %shard_map.59 = (f32[16,8,256]{2,1,0:T(8,128)S(1)}, f32[16,8,256]{2,1,0:T(8,128)S(1)}) custom-call(s32[4,8,1024]{2,1,0:T(8,128)S(1)} %copy-done, s32[16,8,256]{2,1,0:T(8,128)S(1)} %copy-done.1, s32[1,1024]{1,0:T(1,128)S(1)} %bitcast.2, f32[1,1024]{1,0:T(1,128)S(1)} %bitcast.3), custom_call_target="tpu_custom_call" | custom-call | tf_op jit(solution)/shard_map/pallas_call | solution.py:480
  68.3 0.7 copy.8
  69.0 0.7 copy.9
Async XLA Ops:
  0.6 0.9 %copy-start = (s32[4,8,1024]{2,1,0:T(8,128)S(1)}, s32[4,8,1024]{2,1,0:T(8,128)}, u32[]{:S(2)}) copy-start(s32[4,8,1024]{2,1,0:T(8,128)} %refs_0_.1) | copy-start | bytes 393220
  1.5 0.9 %copy-start.1 = (s32[16,8,256]{2,1,0:T(8,128)S(1)}, s32[16,8,256]{2,1,0:T(8,128)}, u32[]{:S(2)}) copy-start(s32[16,8,256]{2,1,0:T(8,128)} %refs_1_.1) | copy-start | bytes 393220
  2.4 0.7 copy-start.2
  3.1 0.7 copy-start.3

commit v4 on v3

--- a/solution.py
+++ b/solution.py
@@ -38,6 +38,29 @@
     )
 
 
+def thirds(v):
+    high = v.astype(jnp.bfloat16)
+    rest = v - high.astype(jnp.float32)
+    middle = rest.astype(jnp.bfloat16)
+    return high, middle, (rest - middle.astype(jnp.float32)).astype(jnp.bfloat16)
+
+
+def dot16(a, b):
+    return lax.dot_general(a, b, (((1,), (0,)), ((), ())), preferred_element_type=jnp.float32)
+
+
+def left_mm(a, v):
+    a = a.astype(jnp.bfloat16)
+    high, middle, low = [dot16(a, part) for part in thirds(v)]
+    return high + (middle + low)
+
+
+def right_mm(v, b):
+    b = b.astype(jnp.bfloat16)
+    high, middle, low = [dot16(part, b) for part in thirds(v)]
+    return high + (middle + low)
+
+
 def pick(shape, test, value):
     return jnp.where(test(iota(shape, 0), iota(shape, 1)), jnp.float32(value), jnp.float32(0.0))
 
@@ -73,11 +96,11 @@
 
 
 def coarse2(v, z):
-    return mm(mm(left_coarse(v.shape[0], z), v), right_coarse(v.shape[1]))
+    return right_mm(left_mm(left_coarse(v.shape[0], z), v), right_coarse(v.shape[1]))
 
 
 def fine2(v, z):
-    return mm(mm(left_fine(v.shape[0] * 4, z), v), right_fine(v.shape[1] * 2))
+    return left_mm(left_fine(v.shape[0] * 4, z), right_mm(v, right_fine(v.shape[1] * 2)))
 
 
 def neighbours(v, z, xlo, xhi, edge):
@@ -236,6 +259,9 @@
         rows, ys = v.shape
         sx[phase, 0] = v[rows - z :]
         sx[phase, 1] = v[:z]
+        copies = halo_copies(level, phase)
+        for copy, can_send, _ in copies[:2]:
+            pl.when(can_send)(copy.start)
         lane = iota((8, 128), 1)
         for side, at in ((0, ys - 1), (1, 0)):
             packed = jnp.zeros((8, 128), jnp.float32)
@@ -243,13 +269,14 @@
                 column = jnp.broadcast_to(v[8 * k : 8 * k + 8, at : at + 1], (8, 128))
                 packed = jnp.where(lane == k, column, packed)
             sy[phase, side] = packed
-        for copy, can_send, _ in halo_copies(level, phase):
+            copy, can_send, _ = copies[2 + side]
             pl.when(can_send)(copy.start)
 
     def finish(level, phase):
         hx, hy = (hx0, hy0) if level == 0 else (hx1, hy1)
         rows, ys = (rows0, y) if level == 0 else (rows1, y1)
-        for copy, _, can_recv in halo_copies(level, phase):
+        copies = halo_copies(level, phase)
+        for copy, _, can_recv in copies[2:]:
             pl.when(can_recv)(copy.wait_recv)
         low, high = hy[phase, 0], hy[phase, 1]
         lane = iota((8, ys), 1)
@@ -260,7 +287,10 @@
                 jnp.broadcast_to(low[:, k : k + 1], (8, ys)),
                 jnp.broadcast_to(high[:, k : k + 1], (8, ys)),
             ))
-        return hx[phase, 0], hx[phase, 1], jnp.concatenate(tiles, axis=0)
+        edge = jnp.concatenate(tiles, axis=0)
+        for copy, _, can_recv in copies[:2]:
+            pl.when(can_recv)(copy.wait_recv)
+        return hx[phase, 0], hx[phase, 1], edge
 
     def around(level, phase, w_ref, v, z):
         start(level, phase, v)
@@ -346,7 +376,7 @@
         load.wait()
     src = scattered(cells_in[...], values_in[...], rows0, z0, cx, y)
     to_x = pick((rows0, rows0), lambda i, j: (i >> log2(z0)) + ((i & (z0 - 1)) << log2(cx)) == j, 1.0)
-    open_cells = 1.0 - mm(to_x, flags_in[...].astype(jnp.float32).reshape(rows0, y))
+    open_cells = 1.0 - left_mm(to_x, flags_in[...].astype(jnp.float32).reshape(rows0, y))
     along_z = taper_z(rows0, z0, cx)
     for _, into in slab_copies:
         into.wait_recv()
@@ -379,7 +409,7 @@
     start(0, 0, d0)
     d1 = coarse2(d0, z0)
     start(1, 0, d1)
-    gather_begin(NEWTON, mm(left12, mm(d1, right12a)))
+    gather_begin(NEWTON, left_mm(left12, right_mm(d1, right12a)))
     face0 = put_weights(w0, d0, z0, finish(0, 0), 1.0)
     face1 = put_weights(w1, d1, z1, finish(1, 0), 0.25)
     gather_pass(NEWTON)
@@ -403,10 +433,10 @@
         v1 = step1 * t1
         start(1, n + 1, v1)
         inner1 = laplace(w1, v1, z1, NO_HALO)
-        c1_part = mm(c1, right12b)
+        c1_part = right_mm(c1, right12b)
         xlo1, xhi1, edge1 = finish(1, n + 1)
         res1 = t1 - rim_part(w1, inner1, z1, (xlo1, xhi1, edge1)) - c1 * v1
-        message = mm(left12, mm(res1, right12a) + c1_part)
+        message = left_mm(left12, right_mm(res1, right12a) + c1_part)
         gather_begin(n, message)
         gather_pass(n)
         gather_end(n)
@@ -437,23 +467,23 @@
             lambda i, j: ((j == 0) & (i == s * y2 - 1)) | ((j == y1 - 1) & (i == s * y2 + y2)),
             1.0,
         )
-        near_mine = mm(near, mine)
+        near_mine = right_mm(near, mine)
         up = left_fine(rows1, z1)
-        v1 = v1 + mm(up, near_mine[r2 : 2 * r2])
-        xlo1 = xlo1 + mm(up, near_mine[0:r2])[rows1 - z1 :]
-        xhi1 = xhi1 + mm(up, near_mine[2 * r2 :])[:z1]
-        edge1 = edge1 + mm(up, mm(near[r2 : 2 * r2], rims))
+        v1 = v1 + left_mm(up, near_mine[r2 : 2 * r2])
+        xlo1 = xlo1 + left_mm(up, near_mine[0:r2])[rows1 - z1 :]
+        xhi1 = xhi1 + left_mm(up, near_mine[2 * r2 :])[:z1]
+        edge1 = edge1 + left_mm(up, right_mm(near[r2 : 2 * r2], rims))
         v1 = v1 + step1 * (t1 - laplace(w1, v1, z1, (xlo1, xhi1, edge1)) - c1 * v1)
         v0 = v0 + fine2(v1, z0)
         v0 = v0 + step0 * (target - around(0, 3 * n + 2, w0, v0, z0) - c0 * v0)
         pot = v0 if n == 0 else pot + v0
     start(0, 3 * NEWTON, pot)
     from_x = pick((rows0, rows0), lambda i, j: (j >> log2(z0)) + ((j & (z0 - 1)) << log2(cx)) == i, 1.0)
-    pot_ref[...] = mm(from_x, pot).reshape(nz, cx, y)
+    pot_ref[...] = left_mm(from_x, pot).reshape(nz, cx, y)
     sh, _ = sinh_cosh(pot)
     inner = laplace(w0, pot, z0, NO_HALO) + rb * sh - src
     misfit = rim_part(w0, inner, z0, finish(0, 3 * NEWTON))
-    mis_ref[...] = mm(from_x, misfit).reshape(nz, cx, y)
+    mis_ref[...] = left_mm(from_x, misfit).reshape(nz, cx, y)
 
     for out, _ in slab_copies:
         out.wait_send()

time: 69.9 us -> 68.5 us (0.980)
  Pallas kernels: 64.5 us -> 63.1 us
    pallas_call x1, Pallas kernels: 64.5 us -> 63.1 us  [per_device(): pl.pallas_call(lambda *refs: solver(slabs, bulks, nz, cx, y, *refs), out_...]
where the time goes in v4:
time: 68.5 us; the launch traced here: 68.3 us
  Pallas kernels  63.1 us (92%)
  local copies, waits for them, and re-layouts  4.49 us (7%)
    pallas_call x1, Pallas kernels, per_device(): pl.pallas_call(lambda *refs: solver(slabs, bulks, nz, cx, y, *refs), out_...  63.1 us
    unnamed x10, local copies, waits for them, and re-layouts  4.49 us

profile of v4, /device:TPU:0, one launch (start us, length us, event | category | flops | bytes accessed | tf_op | source)
XLA Modules:
  0.0 68.3 jit_solution(8398711546293327101)
XLA Ops:
  0.6 0.0 copy-start
  0.6 0.9 %copy-done = s32[4,8,1024]{2,1,0:T(8,128)S(1)} copy-done((s32[4,8,1024]{2,1,0:T(8,128)S(1)}, s32[4,8,1024]{2,1,0:T(8,128)}, u32[]{:S(2)}) %copy-start) | copy-done | bytes 131096
  1.5 0.0 copy-start.1
  1.5 0.9 %copy-done.1 = s32[16,8,256]{2,1,0:T(8,128)S(1)} copy-done((s32[16,8,256]{2,1,0:T(8,128)S(1)}, s32[16,8,256]{2,1,0:T(8,128)}, u32[]{:S(2)}) %copy-start.1) | copy-done | bytes 131096
  2.4 0.0 copy-start.2
  2.4 0.7 %copy-done.2 = s32[1024]{0:T(1024)S(1)} copy-done((s32[1024]{0:T(1024)S(1)}, s32[1024]{0:T(1024)}, u32[]{:S(2)}) %copy-start.2) | copy-done | bytes 4120
  3.1 0.0 copy-start.3
  3.1 0.7 %copy-done.3 = f32[1024]{0:T(1024)S(1)} copy-done((f32[1024]{0:T(1024)S(1)}, f32[1024]{0:T(1024)}, u32[]{:S(2)}) %copy-start.3) | copy-done | bytes 4120
  3.8 63.1 %shard_map.59 = (f32[16,8,256]{2,1,0:T(8,128)S(1)}, f32[16,8,256]{2,1,0:T(8,128)S(1)}) custom-call(s32[4,8,1024]{2,1,0:T(8,128)S(1)} %copy-done, s32[16,8,256]{2,1,0:T(8,128)S(1)} %copy-done.1, s32[1,1024]{1,0:T(1,128)S(1)} %bitcast.2, f32[1,1024]{1,0:T(1,128)S(1)} %bitcast.3), custom_call_target="tpu_custom_call" | custom-call | tf_op jit(solution)/shard_map/pallas_call | solution.py:510
  67.0 0.7 copy.8
  67.6 0.7 copy.9
Async XLA Ops:
  0.6 0.9 %copy-start = (s32[4,8,1024]{2,1,0:T(8,128)S(1)}, s32[4,8,1024]{2,1,0:T(8,128)}, u32[]{:S(2)}) copy-start(s32[4,8,1024]{2,1,0:T(8,128)} %refs_0_.1) | copy-start | bytes 393220
  1.5 0.9 %copy-start.1 = (s32[16,8,256]{2,1,0:T(8,128)S(1)}, s32[16,8,256]{2,1,0:T(8,128)}, u32[]{:S(2)}) copy-start(s32[16,8,256]{2,1,0:T(8,128)} %refs_1_.1) | copy-start | bytes 393220
  2.4 0.7 %copy-start.2 = (s32[1024]{0:T(1024)S(1)}, s32[1024]{0:T(1024)}, u32[]{:S(2)}) copy-start(s32[1024]{0:T(1024)} %param.6) | copy-start | bytes 12292
  3.1 0.7 %copy-start.3 = (f32[1024]{0:T(1024)S(1)}, f32[1024]{0:T(1024)}, u32[]{:S(2)}) copy-start(f32[1024]{0:T(1024)} %param.7) | copy-start | bytes 12292
